TPU v7x, 768 devices: a whole 4x8x12 slice. The times are simulated.
768 devices in a mesh: span: 96 (over z, x, core), chord: 8 (over y).
Axes of the slice: x: 4, y: 8, z: 12, core: 2. Of those that a mesh axis runs over, the one named last changes fastest.
Arguments:
- displacement: bfloat16 [96, 8, 1024, 128], P('span', 'chord'), may hold values from -12 to 12
- packed_blocks: bfloat16 [96, 8, 1024, 1024], P('span', 'chord'), as said below
- flex_scale: float32 [96, 8, 1024], P('span', 'chord'), may hold values from 0.5 to 2
- dirichlet_scale: float32 [96, 8, 1024], P('span', 'chord'), may hold values from 0.5 to 2
- dirichlet_diag: bfloat16 [96, 8, 1024], P('span', 'chord'), may hold values from 1.1953125 to 2.5
- link_rows: int32 [96, 8, 4, 256], P('span', 'chord'), may hold values from 0 to 1023, as said below
- link_signs: int32 [96, 8, 4, 256], P('span', 'chord'), may hold values from -1 to 1, as said below
- link_counts: int32 [96, 8, 4], P('span', 'chord'), may hold values from 0 to 256, as said below
Outputs:
- multipliers: float32 [96, 8, 1024, 128], P('span', 'chord')
- residual: float32 [96, 8, 1024, 128], P('span', 'chord')
Inputs may be any that keep to these rules, and one draw needn't show every extreme that they name: `link_rows`: for each subdomain the 4 x 256 entries name every row 0 to 1023 exactly once. `link_counts`: each count equals the count of the opposite direction on the neighbour's side; it is 0 at the edges of the mesh and toward unlisted neighbours, otherwise at least 64; some subdomain uses all 256 slots toward a span neighbour and some toward a chord neighbour. `link_signs`: every entry is 1 or -1; slot p toward a neighbour holds the opposite sign of slot p of the opposite direction on that neighbour. `packed_blocks`: each block's diagonal lies between 1.2 and 2.5.
All inputs are finite; a program needn't handle non-finite values.
Results may differ from a plain program's by a relative error of at most 0.0065.
Values may be sent and summed in bfloat16 or wider, within the bound.
No kernel may reach another device: no remote copies, remote signals or barrier semaphores. Data moves between devices by JAX's collectives and lax.ppermute only.
A program may use at most 32 MiB of HBM per device.

v0:
```python
import jax
import jax.numpy as jnp
from jax import lax
from jax.sharding import PartitionSpec as P


def extended(block, sides, width):
    for axis, dim in sides:
        count = lax.axis_size(axis)
        forward = [(i, i + 1) for i in range(count - 1)]
        backward = [(target, source) for source, target in forward]
        low = lax.ppermute(
            lax.slice_in_dim(block, block.shape[dim] - width, None, axis=dim), axis, forward
        )
        high = lax.ppermute(lax.slice_in_dim(block, 0, width, axis=dim), axis, backward)
        block = jnp.concatenate([low, block, high], axis=dim)
    return block


def build_blocks(packed, diag):
    size = packed.shape[0]
    row_ids = lax.broadcasted_iota(jnp.int32, (size, size), 0)
    col_ids = lax.broadcasted_iota(jnp.int32, (size, size), 1)
    mirror = packed.T
    flex_block = jnp.where(col_ids >= row_ids, packed, mirror)
    lower = jnp.where(row_ids > col_ids, packed, mirror)
    dirichlet_block = jnp.where(row_ids == col_ids, diag[:, None], lower)
    return (flex_block, dirichlet_block)


def local_term(block, scale, sign_row, field):
    operand = (scale[:, None] * sign_row[:, None] * field).astype(jnp.bfloat16)
    product = jnp.dot(block, operand, preferred_element_type=jnp.float32)
    return (sign_row[:, None] * scale[:, None] * product).astype(jnp.bfloat16)


def exchange_rows(term, flat_rows, valid, slots):
    width = term.shape[1]
    sent = jnp.take(term, flat_rows, axis=0).reshape(4, slots, width)
    sent = jnp.where(valid[:, :, None], sent, jnp.zeros_like(sent))
    span_in = extended(sent[0:2], (("span", 0),), 1)
    chord_in = extended(sent[2:4], (("chord", 0),), 1)
    received = jnp.stack([span_in[0], span_in[3], chord_in[0], chord_in[3]])
    received = jnp.where(valid[:, :, None], received, jnp.zeros_like(received))
    total = sent.astype(jnp.float32) + received.astype(jnp.float32)
    return (
        jnp.zeros((term.shape[0], width), jnp.float32)
        .at[flat_rows]
        .set(total.reshape(4 * slots, width))
    )


def local_gram(left, right):
    return lax.dot_general(
        left,
        right,
        (((0,), (0,)), ((), ())),
        precision=lax.Precision.HIGHEST,
        preferred_element_type=jnp.float32,
    )


def gram(left, right):
    return 0.5 * lax.psum(local_gram(left, right), ("span", "chord"))


def spd_solve(matrix, rhs):
    factor = jnp.linalg.cholesky(matrix)
    return jax.scipy.linalg.cho_solve((factor, True), rhs)


def mat_right(field, small):
    return jnp.dot(
        field, small, precision=lax.Precision.HIGHEST, preferred_element_type=jnp.float32
    )


def shards(
    displacement,
    packed_blocks,
    flex_scale,
    dirichlet_scale,
    dirichlet_diag,
    link_rows,
    link_signs,
    link_counts,
):
    rows_local = link_rows[0, 0]
    slots = rows_local.shape[1]
    flat_rows = rows_local.reshape(-1)
    valid = lax.broadcasted_iota(jnp.int32, rows_local.shape, 1) < link_counts[0, 0][:, None]
    sign_values = jnp.where(valid, link_signs[0, 0], 0).astype(jnp.float32).reshape(-1)
    sign_row = jnp.zeros((packed_blocks.shape[2],), jnp.float32).at[flat_rows].set(sign_values)
    flex_block, dirichlet_block = build_blocks(packed_blocks[0, 0], dirichlet_diag[0, 0])
    fscale = flex_scale[0, 0]
    dscale = dirichlet_scale[0, 0]
    gap_term = (sign_row[:, None] * displacement[0, 0].astype(jnp.float32)).astype(jnp.bfloat16)
    right = exchange_rows(gap_term, flat_rows, valid, slots)
    residual = right
    precond = exchange_rows(
        local_term(dirichlet_block, dscale, sign_row, residual), flat_rows, valid, slots
    )
    gamma = gram(precond, residual)
    image = exchange_rows(
        local_term(flex_block, fscale, sign_row, precond), flat_rows, valid, slots
    )
    curv = gram(precond, image)
    alpha = spd_solve(curv, gamma)
    multipliers = mat_right(precond, alpha)
    residual = residual - mat_right(image, alpha)
    return (multipliers[None, None], residual[None, None])


def solution(mesh):
    return jax.shard_map(
        shards,
        mesh=mesh,
        in_specs=(
            P("span", "chord", None, None),
            P("span", "chord", None, None),
            P("span", "chord", None),
            P("span", "chord", None),
            P("span", "chord", None),
            P("span", "chord", None, None),
            P("span", "chord", None, None),
            P("span", "chord", None),
        ),
        out_specs=(P("span", "chord", None, None), P("span", "chord", None, None)),
        check_vma=False,
    )
```

profile of v0, /device:TPU:4, one launch (start us, length us, event | category | flops | bytes accessed | tf_op | source)
XLA Modules:
  0.0 611.1 jit_solution(3740190900162166840)
XLA Ops:
  10.1 4.3 scatter_custom_fusion
  15.6 3.2 gather_fusion
  19.2 1.9 collective-permute-start
  22.5 4.5 collective-permute-start.2
  27.0 3.1 collective-permute-start.1
  30.2 2.6 copy.10
  33.1 4.0 scatter_custom_fusion.1
  37.0 2.4 fusion.18
  39.5 3.2 gather_fusion.1
  43.1 2.4 collective-permute-start.4
  46.9 4.5 collective-permute-start.6
  51.4 2.6 collective-permute-start.5
  54.0 1.9 collective-permute-done.5
  56.8 4.3 scatter_custom_fusion.2
  61.1 2.4 fusion.15
  63.6 3.2 gather_fusion.2
  67.2 5.8 collective-permute-start.8
  74.3 4.5 collective-permute-start.10
  78.9 2.1 collective-permute-start.9
  81.0 1.6 fusion.68
  83.0 4.0 scatter_custom_fusion.3
  88.6 486.9 %all-reduce.3.cloned.1.call-done = (f32[128,128]{1,0:T(8,128)}, f32[128,128]{1,0:T(8,128)}) async-done(((f32[128,128]{1,0:T(8,128)}, f32[128,128]{1,0:T(8,128)}), (f32[128,128]{1,0:T(8,128)}, f32[128,128]{1,0:T(8,128)})) %all-reduce.3.cloned.1.call-update) | async-done | bytes 131088 | tf_op jit(solution)/shard_map/psum | solution.py:64
  577.3 11.7 %cholesky.16 = f32[128,128]{1,0:T(8,128)S(1)} custom-call(f32[128,128]{1,0:T(8,128)S(1)} %fusion.54), custom_call_target="Cholesky" | custom-call | tf_op jit(solution)/shard_map/jit(cholesky)/cholesky | solution.py:68
  590.3 9.8 %custom-call.10 = f32[1,128,128]{1,2,0:T(8,128)S(1)} custom-call(f32[1,128,128]{2,1,0:T(8,128)S(1)} %fusion.49), custom_call_target="InvertDiagBlocksLowerTriangular" | custom-call | tf_op jit(solution)/shard_map/jit(_cho_solve)/triangular_solve | solution.py:69
  (62 shorter events, 19.6 us)
Async XLA Ops:
  7.2 568.3 %all-reduce.3.cloned.1.call-start = ((), (), s32[]{:S(2)}) async-start(), calls=%async_computation | async-start | bytes 262144 | tf_op jit(solution)/shard_map/psum | solution.py:64
  15.5 14.6 %copy-start.1 = (f32[1,1,1024]{2,1,0:T(1,128)S(1)}, f32[1,1,1024]{2,1,0:T(1,128)}, u32[]{:S(2)}) copy-start(f32[1,1,1024]{2,1,0:T(1,128)} %param.12) | copy-start | bytes 12292
  15.6 14.6 %copy-start.2 = (f32[1,1,1024]{2,1,0:T(1,128)S(1)}, f32[1,1,1024]{2,1,0:T(1,128)}, u32[]{:S(2)}) copy-start(f32[1,1,1024]{2,1,0:T(1,128)} %param.13) | copy-start | bytes 12292
  15.6 14.6 %copy-start = (bf16[1,1,1024,1024]{3,2,1,0:T(8,128)(2,1)S(1)}, bf16[1,1,1024,1024]{3,2,1,0:T(8,128)(2,1)}, u32[]{:S(2)}) copy-start(bf16[1,1,1024,1024]{3,2,1,0:T(8,128)(2,1)} %param.11) | copy-start | bytes 6291460
  19.2 13.5 %collective-permute-start = (bf16[1,256,128]{2,1,0:T(8,128)(2,1)S(1)}, bf16[1,256,128]{2,1,0:T(8,128)(2,1)S(1)}, u32[]{:S(2)}, u32[]{:S(2)}) collective-permute-start(bf16[1,256,128]{2,1,0:T(8,128)(2,1)S(1)} %get-tuple-element.13), channel_id=1, source_target_pairs={{0,8},{8,16},{16,24},{24,32},{32,40},{40,48},{48,56},{56,64},{64,7... | collective-permute-start | bytes 196616 | tf_op jit(solution)/shard_map/ppermute | solution.py:12
  21.2 11.6 %collective-permute-start.3 = (bf16[1,256,128]{2,1,0:T(8,128)(2,1)S(1)}, bf16[1,256,128]{2,1,0:T(8,128)(2,1)S(1)}, u32[]{:S(2)}, u32[]{:S(2)}) collective-permute-start(bf16[1,256,128]{2,1,0:T(8,128)(2,1)S(1)} %get-tuple-element.14), channel_id=1, source_target_pairs={{1,0},{2,1},{3,2},{4,3},{5,4},{6,5},{7,6},{9,8},{10,9},{11,10},{12... | collective-permute-start | bytes 196616 | tf_op jit(solution)/shard_map/ppermute | solution.py:15
  22.5 10.3 %collective-permute-start.2 = (bf16[1,256,128]{2,1,0:T(8,128)(2,1)S(1)}, bf16[1,256,128]{2,1,0:T(8,128)(2,1)S(1)}, u32[]{:S(2)}, u32[]{:S(2)}) collective-permute-start(bf16[1,256,128]{2,1,0:T(8,128)(2,1)S(1)} %get-tuple-element.15), channel_id=1, source_target_pairs={{0,1},{1,2},{2,3},{3,4},{4,5},{5,6},{6,7},{8,9},{9,10},{10,11},{11... | collective-permute-start | bytes 196616 | tf_op jit(solution)/shard_map/ppermute | solution.py:12
  27.0 5.8 collective-permute-start.1
  30.2 2.6 copy-start.3
  43.1 10.9 %collective-permute-start.4 = (bf16[1,256,128]{2,1,0:T(8,128)(2,1)S(1)}, bf16[1,256,128]{2,1,0:T(8,128)(2,1)S(1)}, u32[]{:S(2)}, u32[]{:S(2)}) collective-permute-start(bf16[1,256,128]{2,1,0:T(8,128)(2,1)S(1)} %get-tuple-element.9), channel_id=1, source_target_pairs={{0,8},{8,16},{16,24},{24,32},{32,40},{40,48},{48,56},{56,64},{64,7... | collective-permute-start | bytes 196616 | tf_op jit(solution)/shard_map/ppermute | solution.py:12
  45.6 8.4 %collective-permute-start.7 = (bf16[1,256,128]{2,1,0:T(8,128)(2,1)S(1)}, bf16[1,256,128]{2,1,0:T(8,128)(2,1)S(1)}, u32[]{:S(2)}, u32[]{:S(2)}) collective-permute-start(bf16[1,256,128]{2,1,0:T(8,128)(2,1)S(1)} %get-tuple-element.10), channel_id=1, source_target_pairs={{1,0},{2,1},{3,2},{4,3},{5,4},{6,5},{7,6},{9,8},{10,9},{11,10},{12... | collective-permute-start | bytes 196616 | tf_op jit(solution)/shard_map/ppermute | solution.py:15
  46.9 7.2 %collective-permute-start.6 = (bf16[1,256,128]{2,1,0:T(8,128)(2,1)S(1)}, bf16[1,256,128]{2,1,0:T(8,128)(2,1)S(1)}, u32[]{:S(2)}, u32[]{:S(2)}) collective-permute-start(bf16[1,256,128]{2,1,0:T(8,128)(2,1)S(1)} %get-tuple-element.11), channel_id=1, source_target_pairs={{0,1},{1,2},{2,3},{3,4},{4,5},{5,6},{6,7},{8,9},{9,10},{10,11},{11... | collective-permute-start | bytes 196616 | tf_op jit(solution)/shard_map/ppermute | solution.py:12
  51.4 4.5 collective-permute-start.5
  67.2 15.4 %collective-permute-start.8 = (bf16[1,256,128]{2,1,0:T(8,128)(2,1)S(1)}, bf16[1,256,128]{2,1,0:T(8,128)(2,1)S(1)}, u32[]{:S(2)}, u32[]{:S(2)}) collective-permute-start(bf16[1,256,128]{2,1,0:T(8,128)(2,1)S(1)} %get-tuple-element.5), channel_id=1, source_target_pairs={{0,8},{8,16},{16,24},{24,32},{32,40},{40,48},{48,56},{56,64},{64,7... | collective-permute-start | bytes 196616 | tf_op jit(solution)/shard_map/ppermute | solution.py:12
  73.0 9.6 %collective-permute-start.11 = (bf16[1,256,128]{2,1,0:T(8,128)(2,1)S(1)}, bf16[1,256,128]{2,1,0:T(8,128)(2,1)S(1)}, u32[]{:S(2)}, u32[]{:S(2)}) collective-permute-start(bf16[1,256,128]{2,1,0:T(8,128)(2,1)S(1)} %get-tuple-element.6), channel_id=1, source_target_pairs={{1,0},{2,1},{3,2},{4,3},{5,4},{6,5},{7,6},{9,8},{10,9},{11,10},{12... | collective-permute-start | bytes 196616 | tf_op jit(solution)/shard_map/ppermute | solution.py:15
  74.3 8.3 %collective-permute-start.10 = (bf16[1,256,128]{2,1,0:T(8,128)(2,1)S(1)}, bf16[1,256,128]{2,1,0:T(8,128)(2,1)S(1)}, u32[]{:S(2)}, u32[]{:S(2)}) collective-permute-start(bf16[1,256,128]{2,1,0:T(8,128)(2,1)S(1)} %get-tuple-element.7), channel_id=1, source_target_pairs={{0,1},{1,2},{2,3},{3,4},{4,5},{5,6},{6,7},{8,9},{9,10},{10,11},{11... | collective-permute-start | bytes 196616 | tf_op jit(solution)/shard_map/ppermute | solution.py:12
  78.9 3.8 collective-permute-start.9
Sparse Core Ops, SparseCore 0:
  88.7 486.7 all-reduce.2
where the time goes:
time: 612 us; the launch traced here: 611 us
  waiting for transfers between devices  489 us (80%)
  other arithmetic  41.3 us (7%)
  starting transfers between devices  35.5 us (6%)
  local copies, waits for them, and re-layouts  18.8 us (3%)
  between operations  14.5 us (2%)
  matrix products  12.1 us (2%)
    psum x1, waiting for transfers between devices, gram(): return 0.5 * lax.psum(local_gram(left, right), ('span', 'chord'))  487 us
    ppermute x6, starting transfers between devices, extended(): lax.ppermute(lax.slice_in_dim(block, block.shape[dim] - width, None, axis...  23.8 us
    another operation x3, other arithmetic, spd_solve(): factor = jnp.linalg.cholesky(matrix)  12.4 us
  transfers between devices with their start and end apart: 13, of which 3 were waited for; matrix products, arithmetic and copies ran while one was open for 1% of the time, Pallas kernels for 0%

commit v1 on v0

v1 whole, which is shorter than its diff:
```python
import functools

import jax
import jax.numpy as jnp
from jax import lax
from jax.experimental import pallas as pl
from jax.experimental.pallas import tpu as pltpu
from jax.sharding import Mesh, PartitionSpec as P

X_CHIPS, CORES = 4, 2
SPAN = ("z", "x", "core")
PLANE = ("x", "core", "y")

BF, F32 = jnp.bfloat16, jnp.float32
TILE = 256
VM = pl.BlockSpec(memory_space=pltpu.VMEM)
SM = pl.BlockSpec(memory_space=pltpu.SMEM)


def call(body, outs, in_specs, scratch=(), flops=10**8, moved=4 * 10**6):
    return pl.pallas_call(
        body,
        out_shape=[jax.ShapeDtypeStruct(shape, dtype) for shape, dtype in outs],
        in_specs=in_specs,
        out_specs=[VM] * len(outs),
        scratch_shapes=list(scratch),
        compiler_params=pltpu.CompilerParams(vmem_limit_bytes=16 * 2**20),
        cost_estimate=pl.CostEstimate(flops=flops, bytes_accessed=moved, transcendentals=0),
    )


def mm(a, b):
    return jnp.dot(a, b, preferred_element_type=F32)


def gram_of(a, b):
    return lax.dot_general(a, b, (((0,), (0,)), ((), ())), preferred_element_type=F32)


def columns(pieces):
    return jnp.concatenate([p.astype(F32) for p in pieces], axis=0).T


def pack_kernel(rows, signs, counts, disp, pick, sent):
    slots = rows.shape[3]
    per = slots // 128
    parts = [(d, h) for d in range(4) for h in range(per)]
    row_cols = columns([rows[0, 0, d : d + 1, h * 128 : (h + 1) * 128] for d, h in parts])
    sign_cols = columns([signs[0, 0, d : d + 1, h * 128 : (h + 1) * 128] for d, h in parts])
    row_cols = row_cols.astype(jnp.int32)
    lanes = lax.broadcasted_iota(jnp.int32, (128, pick.shape[1]), 1)
    place = lax.broadcasted_iota(jnp.int32, (128, 1), 0)
    for j, (d, h) in enumerate(parts):
        here = slice(j * 128, (j + 1) * 128)
        pick[here, :] = jnp.where(lanes == row_cols[:, j : j + 1], 1.0, 0.0).astype(BF)
        live = place + h * 128 < counts[0, 0, d]
        sign = jnp.where(live, sign_cols[:, j : j + 1], 0.0)
        sent[here, :] = (sign * mm(pick[here, :], disp[...])).astype(BF)


def build_kernel(rows, signs, counts, disp, packed, diag, put, sign_row, gap, flex, diri, live_sign):
    slots = rows.shape[3]
    size = put.shape[0]
    per = slots // 128
    parts = [(d, h) for d in range(4) for h in range(per)]
    sign_cols = columns([signs[0, 0, d : d + 1, h * 128 : (h + 1) * 128] for d, h in parts])
    place = lax.broadcasted_iota(jnp.int32, (128, 1), 0)
    for j, (d, h) in enumerate(parts):
        live = place + h * 128 < counts[0, 0, d]
        sign = jnp.where(live, sign_cols[:, j : j + 1], 0.0)
        live_sign[j * 128 : (j + 1) * 128, :] = jnp.broadcast_to(sign, (128, 128)).astype(BF)
    down = lax.broadcasted_iota(jnp.int32, (128, slots), 0)
    for i in range(size // 128):
        here = slice(i * 128, (i + 1) * 128)
        for d in range(4):
            hit = down + i * 128 == rows[0, 0, d : d + 1, :]
            put[here, d * slots : (d + 1) * slots] = jnp.where(hit, 1.0, 0.0).astype(BF)
        sign = mm(put[here, :], live_sign[...])
        sign_row[here, :] = sign.astype(BF)
        gap[here, :] = (sign * disp[here, :].astype(F32)).astype(BF)
    r = lax.broadcasted_iota(jnp.int32, (128, 128), 0)
    c = lax.broadcasted_iota(jnp.int32, (128, 128), 1)
    for i in range(size // 128):
        a = slice(i * 128, (i + 1) * 128)
        for j in range(i + 1, size // 128):
            b = slice(j * 128, (j + 1) * 128)
            upper, lower = packed[a, b], packed[b, a]
            flex[a, b] = upper
            flex[b, a] = upper.T
            diri[b, a] = lower
            diri[a, b] = lower.T
        own = packed[a, a].astype(F32)
        turned = own.T
        flex[a, a] = jnp.where(c >= r, own, turned).astype(BF)
        low = jnp.where(r > c, own, turned)
        diri[a, a] = jnp.where(r == c, diag[0, :, a].astype(F32), low).astype(BF)


def apply_kernel(put, pick, block, sign_row, scale, base, r0, r1, r2, r3, partner, term, sent, operand):
    size = put.shape[0]
    scale_cols = columns([scale[0, :, i * 128 : (i + 1) * 128] for i in range(size // 128)])
    factors = []
    for i in range(size // TILE):
        here = slice(i * TILE, (i + 1) * TILE)
        got = None
        for d, r in enumerate((r0, r1, r2, r3)):
            slots = r.shape[0]
            piece = mm(put[here, d * slots : (d + 1) * slots], r[...])
            got = piece if got is None else got + piece
        partner[here, :] = got.astype(BF)
        each = TILE // 128
        column = jnp.concatenate([scale_cols[:, i * each + k : i * each + k + 1] for k in range(each)], axis=0)
        factor = column * sign_row[here, :].astype(F32)
        operand[here, :] = (factor * (base[here, :].astype(F32) + got)).astype(BF)
    for i in range(size // TILE):
        here = slice(i * TILE, (i + 1) * TILE)
        each = TILE // 128
        column = jnp.concatenate([scale_cols[:, i * each + k : i * each + k + 1] for k in range(each)], axis=0)
        factor = column * sign_row[here, :].astype(F32)
        term[here, :] = (factor * mm(block[here, :], operand[...])).astype(BF)
    for i in range(size // TILE):
        here = slice(i * TILE, (i + 1) * TILE)
        sent[here, :] = mm(pick[here, :], term[...]).astype(BF)


def gram_kernel(base, partner, term, out):
    out[...] = gram_of(base[...], term[...]) + gram_of(partner[...], term[...])


def split3(value):
    high = value.astype(BF)
    rest = value - high.astype(F32)
    mid = rest.astype(BF)
    return high, mid, (rest - mid.astype(F32)).astype(BF)


def finish_kernel(put, r0, r1, r2, r3, gap, part0, term1, part1, term2, alpha, mult, resid):
    size = put.shape[0]
    pieces = split3(alpha[...])
    for i in range(size // TILE):
        here = slice(i * TILE, (i + 1) * TILE)
        got = None
        for d, r in enumerate((r0, r1, r2, r3)):
            slots = r.shape[0]
            piece = mm(put[here, d * slots : (d + 1) * slots], r[...])
            got = piece if got is None else got + piece
        got = got.astype(BF)
        step = sum(mm(f, p) for p in pieces[::-1] for f in (term1[here, :], part1[here, :]))
        mult[here, :] = step
        step = sum(mm(f, p) for p in pieces[::-1] for f in (term2[here, :], got))
        resid[here, :] = gap[here, :].astype(F32) + part0[here, :].astype(F32) - step


def exchange(sent, slots, sizes):
    span_count, chord_count = sizes
    up = lambda n: [(i, i + 1) for i in range(n - 1)]
    down = lambda n: [(i + 1, i) for i in range(n - 1)]
    piece = [sent[d * slots : (d + 1) * slots] for d in range(4)]
    return (
        lax.ppermute(piece[1], SPAN, up(span_count)),
        lax.ppermute(piece[0], SPAN, down(span_count)),
        lax.ppermute(piece[3], "y", up(chord_count)),
        lax.ppermute(piece[2], "y", down(chord_count)),
    )


def reduce_all(value):
    rows, width = value.shape
    plane = lax.axis_size(PLANE)
    height = lax.axis_size("z")
    chunks = lax.all_to_all(value.reshape(plane, rows // plane, width), PLANE, 0, 0)
    chunk = jnp.sum(chunks, axis=0)
    layers = lax.all_to_all(jnp.broadcast_to(chunk[None], (height,) + chunk.shape), "z", 0, 0)
    chunk = jnp.sum(layers, axis=0)
    whole = lax.all_to_all(jnp.broadcast_to(chunk[None], (plane,) + chunk.shape), PLANE, 0, 0)
    return whole.reshape(rows, width)


def spd_solve(matrix, rhs):
    factor = jnp.linalg.cholesky(matrix)
    return jax.scipy.linalg.cho_solve((factor, True), rhs)


def shards(sizes, disp, packed, fscale, dscale, diag, rows, signs, counts):
    size, width = disp.shape[2:]
    slots = rows.shape[3]
    disp, packed = disp[0, 0], packed[0, 0]
    field = ((size, width), BF)
    square = ((size, size), BF)
    pick, sent = call(pack_kernel, [square, field], [VM, VM, SM, VM])(rows, signs, counts, disp)
    got0 = exchange(sent, slots, sizes)
    put, sign_row, gap, flex, diri = call(
        build_kernel,
        [square, field, field, square, square],
        [VM, VM, SM, VM, VM, VM],
        [pltpu.VMEM((size, width), BF)],
    )(rows, signs, counts, disp, packed, diag)

    def operate(block, scale, base, got):
        return call(apply_kernel, [field] * 3, [VM] * 10, [pltpu.VMEM((size, width), BF)], flops=8 * 10**8)(
            put, pick, block, sign_row, scale, base, *got
        )

    def local_gram(base, partner, term):
        return call(gram_kernel, [((width, width), F32)], [VM] * 3)(base, partner, term)[0]

    part0, term1, sent = operate(diri, dscale, gap, got0)
    got1 = exchange(sent, slots, sizes)
    gamma = local_gram(gap, part0, term1)
    part1, term2, sent = operate(flex, fscale, term1, got1)
    got2 = exchange(sent, slots, sizes)
    curv = local_gram(term1, part1, term2)
    both = reduce_all(jnp.concatenate([gamma, curv], axis=0))
    alpha = spd_solve(both[width:], both[:width])
    mult, resid = call(finish_kernel, [((size, width), F32)] * 2, [VM] * 11)(
        put, *got2, gap, part0, term1, part1, term2, alpha
    )
    return mult[None, None], resid[None, None]


def solution(mesh):
    span_count, chord_count = mesh.shape["span"], mesh.shape["chord"]
    grid = (span_count // (X_CHIPS * CORES), X_CHIPS, CORES, chord_count)
    fine = Mesh(mesh.devices.reshape(grid), SPAN + ("y",))
    spec = lambda extra: P(SPAN, "y", *([None] * extra))
    return jax.shard_map(
        functools.partial(shards, (span_count, chord_count)),
        mesh=fine,
        in_specs=tuple(spec(n) for n in (2, 2, 1, 1, 1, 2, 2, 1)),
        out_specs=(spec(2), spec(2)),
        check_vma=False,
    )
```

time: 612 us -> 158 us (0.26)
  the two profiles are of different devices: /device:TPU:4 before, /device:TPU:31 now
where the time goes in v1:
time: 158 us; the launch traced here: 156 us
  starting transfers between devices  54.2 us (34%)
  blocking collectives  41.4 us (26%)
  other arithmetic  29.8 us (19%)
  local copies, waits for them, and re-layouts  14.4 us (9%)
  Pallas kernels  12.2 us (8%)
  matrix products  2.2 us (1%)
    all_to_all x1, blocking collectives, reduce_all(): lax.all_to_all(jnp.broadcast_to(chunk[None], (height,) + chunk.shape), 'z...  27.6 us
    ppermute x3, starting transfers between devices, exchange(): lax.ppermute(piece[1], SPAN, up(span_count))  15.3 us
    another operation x3, other arithmetic, spd_solve(): factor = jnp.linalg.cholesky(matrix)  14.8 us
    all_to_all x1, blocking collectives, reduce_all(): lax.all_to_all(value.reshape(plane, rows // plane, width), PLANE, 0, 0)  13.9 us
    another operation x2, other arithmetic, spd_solve(): return jax.scipy.linalg.cho_solve((factor, True), rhs)  13.4 us
    ppermute x3, starting transfers between devices, exchange(): lax.ppermute(piece[3], 'y', up(chord_count))  13.3 us
    all_to_all x1, starting transfers between devices, reduce_all(): lax.all_to_all(jnp.broadcast_to(chunk[None], (plane,) + chunk.shape), PLA...  11.5 us
    unnamed x26, local copies, waits for them, and re-layouts  8.93 us
  transfers between devices with their start and end apart: 13, of which 1 were waited for; matrix products, arithmetic and copies ran while one was open for 23% of the time, Pallas kernels for 2%

profile of v1, /device:TPU:31, one launch (start us, length us, event | category | flops | bytes accessed | tf_op | source)
XLA Modules:
  0.0 156.2 jit_solution(4303707904485744953)
XLA Ops:
  3.6 1.6 %shard_map.96 = (bf16[1024,1024]{1,0:T(8,128)(2,1)S(1)}, bf16[1024,128]{1,0:T(8,128)(2,1)S(1)}) custom-call(s32[1,1,4,256]{3,2,1,0:T(4,128)S(1)} %copy-done.4, s32[1,1,4,256]{3,2,1,0:T(4,128)S(1)} %copy-done.6, s32[1,1,4]{2,1,0:T(1,128)S(1)} %copy-done.11, bf16[1024,128]{1,0:T(8,128)(2,1)S(1)} %bitcast.21), custom_call_target="tpu_custom_call" | custom-call | flops 100000000 | bytes 4000000 | tf_op jit(solution)/shard_map/pallas_call | solution.py:190
  5.3 2.1 %collective-permute-start.3 = (bf16[256,128]{1,0:T(8,128)(2,1)S(1)}, bf16[256,128]{1,0:T(8,128)(2,1)S(1)}, u32[]{:S(2)}, u32[]{:S(2)}) collective-permute-start(bf16[256,128]{1,0:T(8,128)(2,1)S(1)} %get-tuple-element.40), channel_id=1, source_target_pairs={{1,0},{2,1},{3,2},{4,3},{5,4},{6,5},{7,6},{9,8},{10,9},{11,10},{12... | collective-permute-start | bytes 196616 | tf_op jit(solution)/shard_map/ppermute | solution.py:163
  7.4 4.4 %collective-permute-start.2 = (bf16[256,128]{1,0:T(8,128)(2,1)S(1)}, bf16[256,128]{1,0:T(8,128)(2,1)S(1)}, u32[]{:S(2)}, u32[]{:S(2)}) collective-permute-start(bf16[256,128]{1,0:T(8,128)(2,1)S(1)} %get-tuple-element.41), channel_id=1, source_target_pairs={{0,1},{1,2},{2,3},{3,4},{4,5},{5,6},{6,7},{8,9},{9,10},{10,11},{11... | collective-permute-start | bytes 196616 | tf_op jit(solution)/shard_map/ppermute | solution.py:162
  11.8 3.1 %collective-permute-start.1 = (bf16[256,128]{1,0:T(8,128)(2,1)S(1)}, bf16[256,128]{1,0:T(8,128)(2,1)S(1)}, u32[]{:S(2)}, u32[]{:S(2)}) collective-permute-start(bf16[256,128]{1,0:T(8,128)(2,1)S(1)} %get-tuple-element.42), channel_id=1, source_target_pairs={{8,0},{16,8},{24,16},{32,24},{40,32},{48,40},{56,48},{64,56},{72,6... | collective-permute-start | bytes 196616 | tf_op jit(solution)/shard_map/ppermute | solution.py:161
  15.0 4.5 %collective-permute-start = (bf16[256,128]{1,0:T(8,128)(2,1)S(1)}, bf16[256,128]{1,0:T(8,128)(2,1)S(1)}, u32[]{:S(2)}, u32[]{:S(2)}) collective-permute-start(bf16[256,128]{1,0:T(8,128)(2,1)S(1)} %get-tuple-element.43), channel_id=1, source_target_pairs={{0,8},{8,16},{16,24},{24,32},{32,40},{40,48},{48,56},{56,64},{64,7... | collective-permute-start | bytes 196616 | tf_op jit(solution)/shard_map/ppermute | solution.py:160
  24.8 2.3 %shard_map.95 = (bf16[1024,1024]{1,0:T(8,128)(2,1)S(1)}, bf16[1024,128]{1,0:T(8,128)(2,1)S(1)}, bf16[1024,128]{1,0:T(8,128)(2,1)S(1)}, bf16[1024,1024]{1,0:T(8,128)(2,1)S(1)}, bf16[1024,1024]{1,0:T(8,128)(2,1)S(1)}) custom-call(s32[1,1,4,256]{3,2,1,0:T(4,128)S(1)} %copy-done.5, s32[1,1,4,256]{3,2,1,0:T(4,128)S(1)} %copy-done.7, s32[1,1,4]{2,1,0:T(1,128)S(1)} %copy-done.12, ...), custom_call_target="tpu_custom_call" | custom-call | flops 100000000 | bytes 4000000 | tf_op jit(solution)/shard_map/pallas_call | solution.py:192
  27.1 2.0 %shard_map.97 = (bf16[1024,128]{1,0:T(8,128)(2,1)S(1)}, bf16[1024,128]{1,0:T(8,128)(2,1)S(1)}, bf16[1024,128]{1,0:T(8,128)(2,1)S(1)}) custom-call(bf16[1024,1024]{1,0:T(8,128)(2,1)S(1)} %get-tuple-element.17.put, bf16[1024,1024]{1,0:T(8,128)(2,1)S(1)} %get-tuple-element.18.pick, bf16[1024,1024]{1,0:T(8,128)(2,1)S(1)} %get-tuple-element.21.block, ...), custom_call_target="tpu_custom_call" | custom-call | flops 800000000 | bytes 4000000 | tf_op jit(solution)/shard_map/pallas_call | solution.py:200
  29.2 1.9 %collective-permute-start.7 = (bf16[256,128]{1,0:T(8,128)(2,1)S(1)}, bf16[256,128]{1,0:T(8,128)(2,1)S(1)}, u32[]{:S(2)}, u32[]{:S(2)}) collective-permute-start(bf16[256,128]{1,0:T(8,128)(2,1)S(1)} %get-tuple-element.36), channel_id=1, source_target_pairs={{1,0},{2,1},{3,2},{4,3},{5,4},{6,5},{7,6},{9,8},{10,9},{11,10},{12... | collective-permute-start | bytes 196616 | tf_op jit(solution)/shard_map/ppermute | solution.py:163
  31.1 4.6 %collective-permute-start.6 = (bf16[256,128]{1,0:T(8,128)(2,1)S(1)}, bf16[256,128]{1,0:T(8,128)(2,1)S(1)}, u32[]{:S(2)}, u32[]{:S(2)}) collective-permute-start(bf16[256,128]{1,0:T(8,128)(2,1)S(1)} %get-tuple-element.37), channel_id=1, source_target_pairs={{0,1},{1,2},{2,3},{3,4},{4,5},{5,6},{6,7},{8,9},{9,10},{10,11},{11... | collective-permute-start | bytes 196616 | tf_op jit(solution)/shard_map/ppermute | solution.py:162
  35.7 1.9 %collective-permute-start.5 = (bf16[256,128]{1,0:T(8,128)(2,1)S(1)}, bf16[256,128]{1,0:T(8,128)(2,1)S(1)}, u32[]{:S(2)}, u32[]{:S(2)}) collective-permute-start(bf16[256,128]{1,0:T(8,128)(2,1)S(1)} %get-tuple-element.38), channel_id=1, source_target_pairs={{8,0},{16,8},{24,16},{32,24},{40,32},{48,40},{56,48},{64,56},{72,6... | collective-permute-start | bytes 196616 | tf_op jit(solution)/shard_map/ppermute | solution.py:161
  37.6 5.8 %collective-permute-start.4 = (bf16[256,128]{1,0:T(8,128)(2,1)S(1)}, bf16[256,128]{1,0:T(8,128)(2,1)S(1)}, u32[]{:S(2)}, u32[]{:S(2)}) collective-permute-start(bf16[256,128]{1,0:T(8,128)(2,1)S(1)} %get-tuple-element.39), channel_id=1, source_target_pairs={{0,8},{8,16},{16,24},{24,32},{32,40},{40,48},{48,56},{56,64},{64,7... | collective-permute-start | bytes 196616 | tf_op jit(solution)/shard_map/ppermute | solution.py:160
  44.7 2.0 %shard_map.98 = (bf16[1024,128]{1,0:T(8,128)(2,1)S(1)}, bf16[1024,128]{1,0:T(8,128)(2,1)S(1)}, bf16[1024,128]{1,0:T(8,128)(2,1)S(1)}) custom-call(bf16[1024,1024]{1,0:T(8,128)(2,1)S(1)} %get-tuple-element.17.put, bf16[1024,1024]{1,0:T(8,128)(2,1)S(1)} %get-tuple-element.18.pick, bf16[1024,1024]{1,0:T(8,128)(2,1)S(1)} %get-tuple-element.19.block, ...), custom_call_target="tpu_custom_call" | custom-call | flops 800000000 | bytes 4000000 | tf_op jit(solution)/shard_map/pallas_call | solution.py:200
  47.8 13.9 %all_to_all.15 = f32[64,4,128]{2,1,0:T(4,128)S(1)} all-to-all(f32[64,4,128]{2,1,0:T(4,128)S(1)} %bitcast.25), channel_id=1, replica_groups=mesh['z'=12,'x'=4,'core'=2,'y'=8] {'x','core','y'}, dimensions={0} | all-to-all | bytes 262144 | tf_op jit(solution)/shard_map/all_to_all | solution.py:171
  61.8 27.6 %all_to_all.16 = f32[12,4,128]{2,1,0:T(4,128)S(1)} all-to-all(f32[12,4,128]{2,1,0:T(4,128)S(1)} %broadcast_in_dim.10), channel_id=1, replica_groups=mesh['z'=12,'x'=4,'core'=2,'y'=8] {'z'}, dimensions={0} | all-to-all | bytes 49152 | tf_op jit(solution)/shard_map/all_to_all | solution.py:173
  90.0 11.5 %all-to-all-start.2 = ((f32[64,4,128]{2,1,0:T(4,128)}), f32[64,4,128]{2,1,0:T(4,128)}, u32[]{:S(2)}, u32[]{:S(2)}) async-start(f32[64,4,128]{2,1,0:T(4,128)} %broadcast_in_dim.11), calls=%async_computation.2 | async-start | bytes 262144 | tf_op jit(solution)/shard_map/all_to_all | solution.py:175
  101.6 1.7 %fusion.6 = (bf16[256,128]{1,0:T(8,128)(2,1)}, bf16[256,128]{1,0:T(8,128)(2,1)}, bf16[256,128]{1,0:T(8,128)(2,1)}, bf16[256,128]{1,0:T(8,128)(2,1)}) fusion(bf16[1024,128]{1,0:T(8,128)(2,1)} %copy-done.1), kind=kLoop, calls=%fused_computation.13 | loop fusion | bytes 524288 | tf_op jit(solution)/shard_map/slice | solution.py:158
  103.2 2.2 %collective-permute-start.11 = (bf16[256,128]{1,0:T(8,128)(2,1)}, bf16[256,128]{1,0:T(8,128)(2,1)S(1)}, u32[]{:S(2)}, u32[]{:S(2)}) collective-permute-start(bf16[256,128]{1,0:T(8,128)(2,1)} %get-tuple-element.32), channel_id=1, source_target_pairs={{1,0},{2,1},{3,2},{4,3},{5,4},{6,5},{7,6},{9,8},{10,9},{11,10},{12... | collective-permute-start | bytes 196616 | tf_op jit(solution)/shard_map/ppermute | solution.py:163
  105.4 4.3 %collective-permute-start.10 = (bf16[256,128]{1,0:T(8,128)(2,1)}, bf16[256,128]{1,0:T(8,128)(2,1)S(1)}, u32[]{:S(2)}, u32[]{:S(2)}) collective-permute-start(bf16[256,128]{1,0:T(8,128)(2,1)} %get-tuple-element.33), channel_id=1, source_target_pairs={{0,1},{1,2},{2,3},{3,4},{4,5},{5,6},{6,7},{8,9},{9,10},{10,11},{11... | collective-permute-start | bytes 196616 | tf_op jit(solution)/shard_map/ppermute | solution.py:162
  109.7 2.8 %collective-permute-start.9 = (bf16[256,128]{1,0:T(8,128)(2,1)}, bf16[256,128]{1,0:T(8,128)(2,1)}, u32[]{:S(2)}, u32[]{:S(2)}) collective-permute-start(bf16[256,128]{1,0:T(8,128)(2,1)} %get-tuple-element.34), channel_id=1, source_target_pairs={{8,0},{16,8},{24,16},{32,24},{40,32},{48,40},{56,48},{64,56},{72,6... | collective-permute-start | bytes 196616 | tf_op jit(solution)/shard_map/ppermute | solution.py:161
  112.5 5.0 %collective-permute-start.8 = (bf16[256,128]{1,0:T(8,128)(2,1)}, bf16[256,128]{1,0:T(8,128)(2,1)}, u32[]{:S(2)}, u32[]{:S(2)}) collective-permute-start(bf16[256,128]{1,0:T(8,128)(2,1)} %get-tuple-element.35), channel_id=1, source_target_pairs={{0,8},{8,16},{16,24},{24,32},{32,40},{40,48},{48,56},{56,64},{64,7... | collective-permute-start | bytes 196616 | tf_op jit(solution)/shard_map/ppermute | solution.py:160
  122.2 13.2 %cholesky.16 = f32[128,128]{1,0:T(8,128)} custom-call(f32[128,128]{1,0:T(8,128)} %fusion.5), custom_call_target="Cholesky" | custom-call | tf_op jit(solution)/shard_map/jit(cholesky)/cholesky | solution.py:180
  137.0 2.2 %fusion = f32[1,128,128]{2,1,0:T(8,128)} fusion(f32[128,128]{1,0:T(8,128)} %cholesky.16, pred[]{:T(512)} %compare_reduce_fusion), kind=kLoop, calls=%fused_computation.2 | loop fusion | flops 65536 | bytes 131073 | tf_op jit(solution)/shard_map/jit(_cho_solve)/triangular_solve | solution.py:181
  139.1 11.3 %custom-call.10 = f32[1,128,128]{1,2,0:T(8,128)} custom-call(f32[1,128,128]{2,1,0:T(8,128)} %fusion), custom_call_target="InvertDiagBlocksLowerTriangular" | custom-call | tf_op jit(solution)/shard_map/jit(_cho_solve)/triangular_solve | solution.py:181
  152.7 3.5 %shard_map.101 = (f32[1024,128]{1,0:T(8,128)}, f32[1024,128]{1,0:T(8,128)}) custom-call(bf16[1024,1024]{1,0:T(8,128)(2,1)S(1)} %get-tuple-element.17.put, bf16[256,128]{1,0:T(8,128)(2,1)} %collective-permute-done.8.r0, bf16[256,128]{1,0:T(8,128)(2,1)} %collective-permute-done.9.r1, bf16[256,128]{1,0:T(8,128)(2,1)S(1)} %collective-permute-done.10.r2, ...), custom_call_target="tpu_custom_call" | custom-call | flops 100000000 | bytes 4000000 | tf_op jit(solution)/shard_map/pallas_call | solution.py:215
  (55 shorter events, 19.8 us)
Async XLA Ops:
  0.6 1.0 copy-start.2
  1.6 0.7 copy-start.4
  2.3 0.7 copy-start.6
  3.6 23.5 %copy-start.9 = (f32[1,1,1024]{2,1,0:T(1,128)S(1)}, f32[1,1,1024]{2,1,0:T(1,128)}, u32[]{:S(2)}) copy-start(f32[1,1,1024]{2,1,0:T(1,128)} %scale.2) | copy-start | bytes 12292
  5.3 21.8 %collective-permute-start.3 = (bf16[256,128]{1,0:T(8,128)(2,1)S(1)}, bf16[256,128]{1,0:T(8,128)(2,1)S(1)}, u32[]{:S(2)}, u32[]{:S(2)}) collective-permute-start(bf16[256,128]{1,0:T(8,128)(2,1)S(1)} %get-tuple-element.40), channel_id=1, source_target_pairs={{1,0},{2,1},{3,2},{4,3},{5,4},{6,5},{7,6},{9,8},{10,9},{11,10},{12... | collective-permute-start | bytes 196616 | tf_op jit(solution)/shard_map/ppermute | solution.py:163
  7.4 19.7 %collective-permute-start.2 = (bf16[256,128]{1,0:T(8,128)(2,1)S(1)}, bf16[256,128]{1,0:T(8,128)(2,1)S(1)}, u32[]{:S(2)}, u32[]{:S(2)}) collective-permute-start(bf16[256,128]{1,0:T(8,128)(2,1)S(1)} %get-tuple-element.41), channel_id=1, source_target_pairs={{0,1},{1,2},{2,3},{3,4},{4,5},{5,6},{6,7},{8,9},{9,10},{10,11},{11... | collective-permute-start | bytes 196616 | tf_op jit(solution)/shard_map/ppermute | solution.py:162
  11.8 15.3 %collective-permute-start.1 = (bf16[256,128]{1,0:T(8,128)(2,1)S(1)}, bf16[256,128]{1,0:T(8,128)(2,1)S(1)}, u32[]{:S(2)}, u32[]{:S(2)}) collective-permute-start(bf16[256,128]{1,0:T(8,128)(2,1)S(1)} %get-tuple-element.42), channel_id=1, source_target_pairs={{8,0},{16,8},{24,16},{32,24},{40,32},{48,40},{56,48},{64,56},{72,6... | collective-permute-start | bytes 196616 | tf_op jit(solution)/shard_map/ppermute | solution.py:161
  15.0 12.2 %collective-permute-start = (bf16[256,128]{1,0:T(8,128)(2,1)S(1)}, bf16[256,128]{1,0:T(8,128)(2,1)S(1)}, u32[]{:S(2)}, u32[]{:S(2)}) collective-permute-start(bf16[256,128]{1,0:T(8,128)(2,1)S(1)} %get-tuple-element.43), channel_id=1, source_target_pairs={{0,8},{8,16},{16,24},{24,32},{32,40},{40,48},{48,56},{56,64},{64,7... | collective-permute-start | bytes 196616 | tf_op jit(solution)/shard_map/ppermute | solution.py:160
  19.5 1.6 %copy-start = (bf16[1,1,1024,1024]{3,2,1,0:T(8,128)(2,1)S(1)}, bf16[1,1,1024,1024]{3,2,1,0:T(8,128)(2,1)}, u32[]{:S(2)}) copy-start(bf16[1,1,1024,1024]{3,2,1,0:T(8,128)(2,1)} %param.9) | copy-start | bytes 6291460
  21.1 0.9 copy-start.3
  22.0 0.7 copy-start.5
  22.7 0.7 copy-start.7
  23.4 0.7 copy-start.8
  27.1 17.6 %copy-start.10 = (f32[1,1,1024]{2,1,0:T(1,128)S(1)}, f32[1,1,1024]{2,1,0:T(1,128)}, u32[]{:S(2)}) copy-start(f32[1,1,1024]{2,1,0:T(1,128)} %scale.3) | copy-start | bytes 12292
  29.2 14.6 %collective-permute-start.7 = (bf16[256,128]{1,0:T(8,128)(2,1)S(1)}, bf16[256,128]{1,0:T(8,128)(2,1)S(1)}, u32[]{:S(2)}, u32[]{:S(2)}) collective-permute-start(bf16[256,128]{1,0:T(8,128)(2,1)S(1)} %get-tuple-element.36), channel_id=1, source_target_pairs={{1,0},{2,1},{3,2},{4,3},{5,4},{6,5},{7,6},{9,8},{10,9},{11,10},{12... | collective-permute-start | bytes 196616 | tf_op jit(solution)/shard_map/ppermute | solution.py:163
  31.1 12.6 %collective-permute-start.6 = (bf16[256,128]{1,0:T(8,128)(2,1)S(1)}, bf16[256,128]{1,0:T(8,128)(2,1)S(1)}, u32[]{:S(2)}, u32[]{:S(2)}) collective-permute-start(bf16[256,128]{1,0:T(8,128)(2,1)S(1)} %get-tuple-element.37), channel_id=1, source_target_pairs={{0,1},{1,2},{2,3},{3,4},{4,5},{5,6},{6,7},{8,9},{9,10},{10,11},{11... | collective-permute-start | bytes 196616 | tf_op jit(solution)/shard_map/ppermute | solution.py:162
  35.7 8.1 %collective-permute-start.5 = (bf16[256,128]{1,0:T(8,128)(2,1)S(1)}, bf16[256,128]{1,0:T(8,128)(2,1)S(1)}, u32[]{:S(2)}, u32[]{:S(2)}) collective-permute-start(bf16[256,128]{1,0:T(8,128)(2,1)S(1)} %get-tuple-element.38), channel_id=1, source_target_pairs={{8,0},{16,8},{24,16},{32,24},{40,32},{48,40},{56,48},{64,56},{72,6... | collective-permute-start | bytes 196616 | tf_op jit(solution)/shard_map/ppermute | solution.py:161
  37.6 7.1 %collective-permute-start.4 = (bf16[256,128]{1,0:T(8,128)(2,1)S(1)}, bf16[256,128]{1,0:T(8,128)(2,1)S(1)}, u32[]{:S(2)}, u32[]{:S(2)}) collective-permute-start(bf16[256,128]{1,0:T(8,128)(2,1)S(1)} %get-tuple-element.39), channel_id=1, source_target_pairs={{0,8},{8,16},{16,24},{24,32},{32,40},{40,48},{48,56},{56,64},{64,7... | collective-permute-start | bytes 196616 | tf_op jit(solution)/shard_map/ppermute | solution.py:160
  46.7 0.7 copy-start.1
  90.0 27.5 %all-to-all-start.2 = ((f32[64,4,128]{2,1,0:T(4,128)}), f32[64,4,128]{2,1,0:T(4,128)}, u32[]{:S(2)}, u32[]{:S(2)}) async-start(f32[64,4,128]{2,1,0:T(4,128)} %broadcast_in_dim.11), calls=%async_computation.2 | async-start | bytes 262144 | tf_op jit(solution)/shard_map/all_to_all | solution.py:175
  103.2 49.4 %collective-permute-start.11 = (bf16[256,128]{1,0:T(8,128)(2,1)}, bf16[256,128]{1,0:T(8,128)(2,1)S(1)}, u32[]{:S(2)}, u32[]{:S(2)}) collective-permute-start(bf16[256,128]{1,0:T(8,128)(2,1)} %get-tuple-element.32), channel_id=1, source_target_pairs={{1,0},{2,1},{3,2},{4,3},{5,4},{6,5},{7,6},{9,8},{10,9},{11,10},{12... | collective-permute-start | bytes 196616 | tf_op jit(solution)/shard_map/ppermute | solution.py:163
  105.4 47.2 %collective-permute-start.10 = (bf16[256,128]{1,0:T(8,128)(2,1)}, bf16[256,128]{1,0:T(8,128)(2,1)S(1)}, u32[]{:S(2)}, u32[]{:S(2)}) collective-permute-start(bf16[256,128]{1,0:T(8,128)(2,1)} %get-tuple-element.33), channel_id=1, source_target_pairs={{0,1},{1,2},{2,3},{3,4},{4,5},{5,6},{6,7},{8,9},{9,10},{10,11},{11... | collective-permute-start | bytes 196616 | tf_op jit(solution)/shard_map/ppermute | solution.py:162
  109.7 42.9 %collective-permute-start.9 = (bf16[256,128]{1,0:T(8,128)(2,1)}, bf16[256,128]{1,0:T(8,128)(2,1)}, u32[]{:S(2)}, u32[]{:S(2)}) collective-permute-start(bf16[256,128]{1,0:T(8,128)(2,1)} %get-tuple-element.34), channel_id=1, source_target_pairs={{8,0},{16,8},{24,16},{32,24},{40,32},{48,40},{56,48},{64,56},{72,6... | collective-permute-start | bytes 196616 | tf_op jit(solution)/shard_map/ppermute | solution.py:161
  112.5 40.1 %collective-permute-start.8 = (bf16[256,128]{1,0:T(8,128)(2,1)}, bf16[256,128]{1,0:T(8,128)(2,1)}, u32[]{:S(2)}, u32[]{:S(2)}) collective-permute-start(bf16[256,128]{1,0:T(8,128)(2,1)} %get-tuple-element.35), channel_id=1, source_target_pairs={{0,8},{8,16},{16,24},{24,32},{32,40},{40,48},{48,56},{56,64},{64,7... | collective-permute-start | bytes 196616 | tf_op jit(solution)/shard_map/ppermute | solution.py:160
  (2 other events, 1.3 us)

commit v2 on v1

--- a/solution.py
+++ b/solution.py
@@ -13,16 +13,17 @@
 
 BF, F32 = jnp.bfloat16, jnp.float32
 TILE = 256
+STEP = 4
 VM = pl.BlockSpec(memory_space=pltpu.VMEM)
-SM = pl.BlockSpec(memory_space=pltpu.SMEM)
-
-
-def call(body, outs, in_specs, scratch=(), flops=10**8, moved=4 * 10**6):
+HB = pl.BlockSpec(memory_space=pltpu.HBM)
+
+
+def call(body, outs, in_specs, scratch=(), flops=10**8, moved=4 * 10**6, out_spec=VM):
     return pl.pallas_call(
         body,
         out_shape=[jax.ShapeDtypeStruct(shape, dtype) for shape, dtype in outs],
         in_specs=in_specs,
-        out_specs=[VM] * len(outs),
+        out_specs=[out_spec] * len(outs),
         scratch_shapes=list(scratch),
         compiler_params=pltpu.CompilerParams(vmem_limit_bytes=16 * 2**20),
         cost_estimate=pl.CostEstimate(flops=flops, bytes_accessed=moved, transcendentals=0),
@@ -41,34 +42,49 @@
     return jnp.concatenate([p.astype(F32) for p in pieces], axis=0).T
 
 
-def pack_kernel(rows, signs, counts, disp, pick, sent):
-    slots = rows.shape[3]
+def pack_kernel(
+    rows, signs, counts, disp, packed, diag, dscale, fscale,
+    pick, s0, s1, s2, s3, live_sign, rows_v, disp_v, packed_v, diag_v, dscale_v, fscale_v,
+    signs_v, counts_s, sems,
+):
+    moves = [
+        pltpu.make_async_copy(src, dst, sems.at[i])
+        for i, (src, dst) in enumerate(
+            (
+                (rows, rows_v), (signs, signs_v), (counts, counts_s), (disp, disp_v),
+                (packed, packed_v), (diag, diag_v), (dscale, dscale_v), (fscale, fscale_v),
+            )
+        )
+    ]
+    for move in moves:
+        move.start()
+    slots = rows_v.shape[3]
     per = slots // 128
     parts = [(d, h) for d in range(4) for h in range(per)]
-    row_cols = columns([rows[0, 0, d : d + 1, h * 128 : (h + 1) * 128] for d, h in parts])
-    sign_cols = columns([signs[0, 0, d : d + 1, h * 128 : (h + 1) * 128] for d, h in parts])
+    moves[0].wait()
+    row_cols = columns([rows_v[0, 0, d : d + 1, h * 128 : (h + 1) * 128] for d, h in parts])
     row_cols = row_cols.astype(jnp.int32)
+    moves[1].wait()
+    sign_cols = columns([signs_v[0, 0, d : d + 1, h * 128 : (h + 1) * 128] for d, h in parts])
+    moves[2].wait()
+    moves[3].wait()
     lanes = lax.broadcasted_iota(jnp.int32, (128, pick.shape[1]), 1)
     place = lax.broadcasted_iota(jnp.int32, (128, 1), 0)
     for j, (d, h) in enumerate(parts):
         here = slice(j * 128, (j + 1) * 128)
         pick[here, :] = jnp.where(lanes == row_cols[:, j : j + 1], 1.0, 0.0).astype(BF)
-        live = place + h * 128 < counts[0, 0, d]
+        live = place + h * 128 < counts_s[0, 0, d]
         sign = jnp.where(live, sign_cols[:, j : j + 1], 0.0)
-        sent[here, :] = (sign * mm(pick[here, :], disp[...])).astype(BF)
-
-
-def build_kernel(rows, signs, counts, disp, packed, diag, put, sign_row, gap, flex, diri, live_sign):
+        live_sign[here, :] = jnp.broadcast_to(sign, (128, 128)).astype(BF)
+        sent = (s0, s1, s2, s3)[d]
+        sent[h * 128 : (h + 1) * 128, :] = (sign * mm(pick[here, :], disp_v[...])).astype(BF)
+    for move in moves[4:]:
+        move.wait()
+
+
+def build_kernel(rows, live_sign, disp, packed, diag, put, sign_row, gap, flex, diri):
     slots = rows.shape[3]
     size = put.shape[0]
-    per = slots // 128
-    parts = [(d, h) for d in range(4) for h in range(per)]
-    sign_cols = columns([signs[0, 0, d : d + 1, h * 128 : (h + 1) * 128] for d, h in parts])
-    place = lax.broadcasted_iota(jnp.int32, (128, 1), 0)
-    for j, (d, h) in enumerate(parts):
-        live = place + h * 128 < counts[0, 0, d]
-        sign = jnp.where(live, sign_cols[:, j : j + 1], 0.0)
-        live_sign[j * 128 : (j + 1) * 128, :] = jnp.broadcast_to(sign, (128, 128)).astype(BF)
     down = lax.broadcasted_iota(jnp.int32, (128, slots), 0)
     for i in range(size // 128):
         here = slice(i * 128, (i + 1) * 128)
@@ -96,7 +112,7 @@
         diri[a, a] = jnp.where(r == c, diag[0, :, a].astype(F32), low).astype(BF)
 
 
-def apply_kernel(put, pick, block, sign_row, scale, base, r0, r1, r2, r3, partner, term, sent, operand):
+def apply_kernel(put, pick, block, sign_row, scale, base, r0, r1, r2, r3, partner, term, s0, s1, s2, s3, operand):
     size = put.shape[0]
     scale_cols = columns([scale[0, :, i * 128 : (i + 1) * 128] for i in range(size // 128)])
     factors = []
@@ -118,9 +134,9 @@
         column = jnp.concatenate([scale_cols[:, i * each + k : i * each + k + 1] for k in range(each)], axis=0)
         factor = column * sign_row[here, :].astype(F32)
         term[here, :] = (factor * mm(block[here, :], operand[...])).astype(BF)
-    for i in range(size // TILE):
-        here = slice(i * TILE, (i + 1) * TILE)
-        sent[here, :] = mm(pick[here, :], term[...]).astype(BF)
+    for d, sent in enumerate((s0, s1, s2, s3)):
+        slots = sent.shape[0]
+        sent[...] = mm(pick[d * slots : (d + 1) * slots, :], term[...]).astype(BF)
 
 
 def gram_kernel(base, partner, term, out):
@@ -134,28 +150,85 @@
     return high, mid, (rest - mid.astype(F32)).astype(BF)
 
 
-def finish_kernel(put, r0, r1, r2, r3, gap, part0, term1, part1, term2, alpha, mult, resid):
+def small_solve(p, r):
+    n = len(p)
+    if n == 2:
+        scale = 1.0 / (p[0][0] * p[1][1] - p[0][1] * p[1][0])
+        return [
+            (p[1][1] * scale) * r[0] - (p[0][1] * scale) * r[1],
+            (p[0][0] * scale) * r[1] - (p[1][0] * scale) * r[0],
+        ]
+    h = n // 2
+    one, rest = range(h), range(h, n)
+    a = [row[:h] for row in p[:h]]
+    across = [small_solve(a, [p[i][j] for i in one]) for j in rest]
+    u = small_solve(a, r[:h])
+    schur = [[p[i][h + j] - sum(p[i][k] * across[j][k] for k in one) for j in range(n - h)] for i in rest]
+    v = small_solve(schur, [r[i] - sum(p[i][k] * u[k] for k in one) for i in rest])
+    return [u[i] - sum(across[j][i] * v[j] for j in range(n - h)) for i in one] + v
+
+
+def solve_kernel(both, alpha):
+    width = alpha.shape[0]
+    count = width // 8
+    rows = both.shape[1]
+
+    def tile(t):
+        if rows >= 8:
+            return both[t * 8 // rows, t * 8 % rows : t * 8 % rows + 8]
+        return jnp.concatenate([both[t * (8 // rows) + k] for k in range(8 // rows)], axis=0)
+
+    g = [tile(t) for t in range(count)]
+    curv = jnp.concatenate([tile(count + t) for t in range(count)], axis=0)
+    curv = (curv + curv.T) * 0.5
+    a = [curv[8 * t : 8 * t + 8, :] for t in range(count)]
+    spot = lax.broadcasted_iota(jnp.int32, (8, width), 0)
+    for j in range(0, width, STEP):
+        cols = [[jnp.broadcast_to(a[t][:, j + k : j + k + 1], (8, width)) for k in range(STEP)] for t in range(count)]
+        own, r0 = j // 8, j % 8
+        row = lambda x, k: jnp.broadcast_to(x[r0 + k : r0 + k + 1, :], (8, width))
+        p = [[row(cols[own][l], k) for l in range(STEP)] for k in range(STEP)]
+        na = small_solve(p, [row(a[own], k) for k in range(STEP)])
+        ng = small_solve(p, [row(g[own], k) for k in range(STEP)])
+        for t in range(count):
+            ua = a[t] - sum(cols[t][k] * na[k] for k in range(STEP))
+            ug = g[t] - sum(cols[t][k] * ng[k] for k in range(STEP))
+            if t == own:
+                for k in range(STEP):
+                    ua = jnp.where(spot == r0 + k, na[k], ua)
+                    ug = jnp.where(spot == r0 + k, ng[k], ug)
+            a[t], g[t] = ua, ug
+    for t in range(count):
+        alpha[8 * t : 8 * t + 8, :] = g[t]
+
+
+def finish_kernel(put, r0, r1, r2, r3, gap, part0, term1, part1, term2, alpha, mult, resid, mult_v, resid_v, sems):
     size = put.shape[0]
     pieces = split3(alpha[...])
+    moves = []
     for i in range(size // TILE):
         here = slice(i * TILE, (i + 1) * TILE)
+        mult_v[here, :] = sum(mm(f, p) for p in pieces[::-1] for f in (term1[here, :], part1[here, :]))
+        moves.append(pltpu.make_async_copy(mult_v.at[here, :], mult.at[here, :], sems.at[0, i]))
+        moves[-1].start()
         got = None
         for d, r in enumerate((r0, r1, r2, r3)):
             slots = r.shape[0]
             piece = mm(put[here, d * slots : (d + 1) * slots], r[...])
             got = piece if got is None else got + piece
         got = got.astype(BF)
-        step = sum(mm(f, p) for p in pieces[::-1] for f in (term1[here, :], part1[here, :]))
-        mult[here, :] = step
         step = sum(mm(f, p) for p in pieces[::-1] for f in (term2[here, :], got))
-        resid[here, :] = gap[here, :].astype(F32) + part0[here, :].astype(F32) - step
-
-
-def exchange(sent, slots, sizes):
+        resid_v[here, :] = gap[here, :].astype(F32) + part0[here, :].astype(F32) - step
+        moves.append(pltpu.make_async_copy(resid_v.at[here, :], resid.at[here, :], sems.at[1, i]))
+        moves[-1].start()
+    for move in moves:
+        move.wait()
+
+
+def exchange(piece, sizes):
     span_count, chord_count = sizes
     up = lambda n: [(i, i + 1) for i in range(n - 1)]
     down = lambda n: [(i + 1, i) for i in range(n - 1)]
-    piece = [sent[d * slots : (d + 1) * slots] for d in range(4)]
     return (
         lax.ppermute(piece[1], SPAN, up(span_count)),
         lax.ppermute(piece[0], SPAN, down(span_count)),
@@ -173,48 +246,52 @@
     layers = lax.all_to_all(jnp.broadcast_to(chunk[None], (height,) + chunk.shape), "z", 0, 0)
     chunk = jnp.sum(layers, axis=0)
     whole = lax.all_to_all(jnp.broadcast_to(chunk[None], (plane,) + chunk.shape), PLANE, 0, 0)
-    return whole.reshape(rows, width)
-
-
-def spd_solve(matrix, rhs):
-    factor = jnp.linalg.cholesky(matrix)
-    return jax.scipy.linalg.cho_solve((factor, True), rhs)
+    return whole
 
 
 def shards(sizes, disp, packed, fscale, dscale, diag, rows, signs, counts):
     size, width = disp.shape[2:]
     slots = rows.shape[3]
     disp, packed = disp[0, 0], packed[0, 0]
-    field = ((size, width), BF)
-    square = ((size, size), BF)
-    pick, sent = call(pack_kernel, [square, field], [VM, VM, SM, VM])(rows, signs, counts, disp)
-    got0 = exchange(sent, slots, sizes)
-    put, sign_row, gap, flex, diri = call(
-        build_kernel,
-        [square, field, field, square, square],
-        [VM, VM, SM, VM, VM, VM],
-        [pltpu.VMEM((size, width), BF)],
-    )(rows, signs, counts, disp, packed, diag)
+    field, square, piece = ((size, width), BF), ((size, size), BF), ((slots, width), BF)
+    like = lambda x: (x.shape, x.dtype)
+    pick, *out = call(
+        pack_kernel,
+        [square] + [piece] * 4 + [field] + [like(x) for x in (rows, disp, packed, diag, dscale, fscale)],
+        [HB] * 8,
+        [pltpu.VMEM(signs.shape, signs.dtype), pltpu.SMEM(counts.shape, counts.dtype), pltpu.SemaphoreType.DMA((8,))],
+    )(*(pltpu.with_memory_space_constraint(x, pltpu.HBM) for x in (rows, signs, counts, disp, packed, diag, dscale, fscale)))
+    live_sign, rows, disp, packed, diag, dscale, fscale = out[4:]
+    got0 = exchange(out[:4], sizes)
+    put, sign_row, gap, flex, diri = call(build_kernel, [square, field, field, square, square], [VM] * 5)(
+        rows, live_sign, disp, packed, diag
+    )
 
     def operate(block, scale, base, got):
-        return call(apply_kernel, [field] * 3, [VM] * 10, [pltpu.VMEM((size, width), BF)], flops=8 * 10**8)(
-            put, pick, block, sign_row, scale, base, *got
-        )
+        part, term, *sent = call(
+            apply_kernel, [field] * 2 + [piece] * 4, [VM] * 10, [pltpu.VMEM((size, width), BF)], flops=8 * 10**8
+        )(put, pick, block, sign_row, scale, base, *got)
+        return part, term, sent
 
     def local_gram(base, partner, term):
         return call(gram_kernel, [((width, width), F32)], [VM] * 3)(base, partner, term)[0]
 
     part0, term1, sent = operate(diri, dscale, gap, got0)
-    got1 = exchange(sent, slots, sizes)
+    got1 = exchange(sent, sizes)
     gamma = local_gram(gap, part0, term1)
     part1, term2, sent = operate(flex, fscale, term1, got1)
-    got2 = exchange(sent, slots, sizes)
+    got2 = exchange(sent, sizes)
     curv = local_gram(term1, part1, term2)
     both = reduce_all(jnp.concatenate([gamma, curv], axis=0))
-    alpha = spd_solve(both[width:], both[:width])
-    mult, resid = call(finish_kernel, [((size, width), F32)] * 2, [VM] * 11)(
-        put, *got2, gap, part0, term1, part1, term2, alpha
-    )
+    alpha = call(solve_kernel, [((width, width), F32)], [VM])(both)[0]
+    whole = ((size, width), F32)
+    mult, resid = call(
+        finish_kernel,
+        [whole] * 2,
+        [VM] * 11,
+        [pltpu.VMEM(*whole), pltpu.VMEM(*whole), pltpu.SemaphoreType.DMA((2, size // TILE))],
+        out_spec=HB,
+    )(put, *got2, gap, part0, term1, part1, term2, alpha)
     return mult[None, None], resid[None, None]
 
 

time: 158 us -> 118 us (0.75)
  the two profiles are of different devices: /device:TPU:31 before, /device:TPU:96 now
where the time goes in v2:
time: 118 us
  starting transfers between devices  53.5 us (45%)
  blocking collectives  40 us (34%)
  Pallas kernels  20.1 us (17%)
  waiting for transfers between devices  1.96 us (2%)
    all_to_all x1, blocking collectives, reduce_all(): lax.all_to_all(jnp.broadcast_to(chunk[None], (height,) + chunk.shape), 'z...  24.8 us
    ppermute x3, starting transfers between devices, exchange(): lax.ppermute(piece[0], SPAN, down(span_count))  17.1 us
    all_to_all x1, blocking collectives, reduce_all(): lax.all_to_all(value.reshape(plane, rows // plane, width), PLANE, 0, 0)  15.2 us
    ppermute x3, starting transfers between devices, exchange(): lax.ppermute(piece[2], 'y', down(chord_count))  14.2 us
    all_to_all x1, starting transfers between devices, reduce_all(): lax.all_to_all(jnp.broadcast_to(chunk[None], (plane,) + chunk.shape), PLA...  8.83 us
    pallas_call x1, Pallas kernels, shards(): alpha = call(solve_kernel, [((width, width), F32)], [VM])(both)[0]  8.09 us
    ppermute x3, starting transfers between devices, exchange(): lax.ppermute(piece[3], 'y', up(chord_count))  7.45 us
    ppermute x3, starting transfers between devices, exchange(): lax.ppermute(piece[1], SPAN, up(span_count))  5.92 us
  transfers between devices with their start and end apart: 13, of which 2 were waited for; matrix products, arithmetic and copies ran while one was open for 0% of the time, Pallas kernels for 8%

profile of v2, /device:TPU:96, one launch (start us, length us, event | category | flops | bytes accessed | tf_op | source)
XLA Modules:
  0.0 117.8 jit_solution(6104133898371480778)
XLA Ops:
  0.6 2.2 %shard_map.95 = (bf16[1024,1024]{1,0:T(8,128)(2,1)S(1)}, bf16[256,128]{1,0:T(8,128)(2,1)S(1)}, bf16[256,128]{1,0:T(8,128)(2,1)S(1)}, bf16[256,128]{1,0:T(8,128)(...) custom-call(s32[1,1,4,256]{3,2,1,0:T(4,128)} %rows.1, ...), custom_call_target="tpu_custom_call" | custom-call | flops 100000000 | bytes 4000000 | tf_op jit(solution)/shard_map/pallas_call | solution.py:258
  2.8 1.9 %collective-permute-start = (bf16[256,128]{1,0:T(8,128)(2,1)S(1)}, bf16[256,128]{1,0:T(8,128)(2,1)S(1)}, u32[]{:S(2)}, u32[]{:S(2)}) collective-permute-start(bf16[256,128]{1,0:T(8,128)(2,1)S(1)} %get-tuple-element.46), channel_id=1, source_target_pairs={{0,8},{8,16},{16,24},{24,32},{32,40},{40,48},{48,56},{56,64},{64,7... | collective-permute-start | bytes 196616 | tf_op jit(solution)/shard_map/ppermute | solution.py:233
  4.7 5.8 %collective-permute-start.1 = (bf16[256,128]{1,0:T(8,128)(2,1)S(1)}, bf16[256,128]{1,0:T(8,128)(2,1)S(1)}, u32[]{:S(2)}, u32[]{:S(2)}) collective-permute-start(bf16[256,128]{1,0:T(8,128)(2,1)S(1)} %get-tuple-element.47), channel_id=1, source_target_pairs={{8,0},{16,8},{24,16},{32,24},{40,32},{48,40},{56,48},{64,56},{72,6... | collective-permute-start | bytes 196616 | tf_op jit(solution)/shard_map/ppermute | solution.py:234
  10.5 2.6 %collective-permute-start.2 = (bf16[256,128]{1,0:T(8,128)(2,1)S(1)}, bf16[256,128]{1,0:T(8,128)(2,1)S(1)}, u32[]{:S(2)}, u32[]{:S(2)}) collective-permute-start(bf16[256,128]{1,0:T(8,128)(2,1)S(1)} %get-tuple-element.48), channel_id=1, source_target_pairs={{0,1},{1,2},{2,3},{3,4},{4,5},{5,6},{6,7},{8,9},{9,10},{10,11},{11... | collective-permute-start | bytes 196616 | tf_op jit(solution)/shard_map/ppermute | solution.py:235
  13.1 4.5 %collective-permute-start.3 = (bf16[256,128]{1,0:T(8,128)(2,1)S(1)}, bf16[256,128]{1,0:T(8,128)(2,1)S(1)}, u32[]{:S(2)}, u32[]{:S(2)}) collective-permute-start(bf16[256,128]{1,0:T(8,128)(2,1)S(1)} %get-tuple-element.49), channel_id=1, source_target_pairs={{1,0},{2,1},{3,2},{4,3},{5,4},{6,5},{7,6},{9,8},{10,9},{11,10},{12... | collective-permute-start | bytes 196616 | tf_op jit(solution)/shard_map/ppermute | solution.py:236
  17.6 1.4 %shard_map.96 = (bf16[1024,1024]{1,0:T(8,128)(2,1)S(1)}, bf16[1024,128]{1,0:T(8,128)(2,1)S(1)}, bf16[1024,128]{1,0:T(8,128)(2,1)S(1)}, bf16[1024,1024]{1,0:T(8,128)(2,1)S(1)}, bf16[1024,1024]{1,0:T(8,128)(2,1)S(1)}) custom-call(s32[1,1,4,256]{3,2,1,0:T(4,128)S(1)} %get-tuple-element.33.rows, bf16[1024,128]{1,0:T(8,128)(2,1)S(1)} %get-tuple-element.34.live_sign, ...), custom_call_target="tpu_custom_call" | custom-call | flops 100000000 | bytes 4000000 | tf_op jit(solution)/shard_map/pallas_call | solution.py:266
  19.0 0.4 collective-permute-done.3.r3
  19.4 2.0 %shard_map.97 = (bf16[1024,128]{1,0:T(8,128)(2,1)S(1)}, bf16[1024,128]{1,0:T(8,128)(2,1)S(1)}, bf16[256,128]{1,0:T(8,128)(2,1)S(1)}, bf16[256,128]{1,0:T(8,128)(...) custom-call(bf16[1024,1024]{1,0:T(8,128)(2,1)S(1)} %get-tuple-element.38.put, ...), custom_call_target="tpu_custom_call" | custom-call | flops 800000000 | bytes 4000000 | tf_op jit(solution)/shard_map/pallas_call | solution.py:271
  21.5 1.9 %collective-permute-start.4 = (bf16[256,128]{1,0:T(8,128)(2,1)S(1)}, bf16[256,128]{1,0:T(8,128)(2,1)S(1)}, u32[]{:S(2)}, u32[]{:S(2)}) collective-permute-start(bf16[256,128]{1,0:T(8,128)(2,1)S(1)} %get-tuple-element.51), channel_id=1, source_target_pairs={{0,8},{8,16},{16,24},{24,32},{32,40},{40,48},{48,56},{56,64},{64,7... | collective-permute-start | bytes 196616 | tf_op jit(solution)/shard_map/ppermute | solution.py:233
  23.4 5.8 %collective-permute-start.5 = (bf16[256,128]{1,0:T(8,128)(2,1)S(1)}, bf16[256,128]{1,0:T(8,128)(2,1)S(1)}, u32[]{:S(2)}, u32[]{:S(2)}) collective-permute-start(bf16[256,128]{1,0:T(8,128)(2,1)S(1)} %get-tuple-element.52), channel_id=1, source_target_pairs={{8,0},{16,8},{24,16},{32,24},{40,32},{48,40},{56,48},{64,56},{72,6... | collective-permute-start | bytes 196616 | tf_op jit(solution)/shard_map/ppermute | solution.py:234
  29.2 2.4 %collective-permute-start.6 = (bf16[256,128]{1,0:T(8,128)(2,1)S(1)}, bf16[256,128]{1,0:T(8,128)(2,1)S(1)}, u32[]{:S(2)}, u32[]{:S(2)}) collective-permute-start(bf16[256,128]{1,0:T(8,128)(2,1)S(1)} %get-tuple-element.53), channel_id=1, source_target_pairs={{0,1},{1,2},{2,3},{3,4},{4,5},{5,6},{6,7},{8,9},{9,10},{10,11},{11... | collective-permute-start | bytes 196616 | tf_op jit(solution)/shard_map/ppermute | solution.py:235
  31.6 5.0 %collective-permute-start.7 = (bf16[256,128]{1,0:T(8,128)(2,1)S(1)}, bf16[256,128]{1,0:T(8,128)(2,1)S(1)}, u32[]{:S(2)}, u32[]{:S(2)}) collective-permute-start(bf16[256,128]{1,0:T(8,128)(2,1)S(1)} %get-tuple-element.54), channel_id=1, source_target_pairs={{1,0},{2,1},{3,2},{4,3},{5,4},{6,5},{7,6},{9,8},{10,9},{11,10},{12... | collective-permute-start | bytes 196616 | tf_op jit(solution)/shard_map/ppermute | solution.py:236
  37.0 1.5 %collective-permute-done.7.r3 = bf16[256,128]{1,0:T(8,128)(2,1)S(1)} collective-permute-done((bf16[256,128]{1,0:T(8,128)(2,1)S(1)}, bf16[256,128]{1,0:T(8,128)(2,1)S(1)}, u32[]{:S(2)}, u32[]{:S(2)}) %collective-permute-start.7) | collective-permute-done | bytes 65568 | tf_op jit(solution)/shard_map/ppermute | solution.py:236
  38.5 2.0 %shard_map.98 = (bf16[1024,128]{1,0:T(8,128)(2,1)S(1)}, bf16[1024,128]{1,0:T(8,128)(2,1)S(1)}, bf16[256,128]{1,0:T(8,128)(2,1)S(1)}, bf16[256,128]{1,0:T(8,128)(...) custom-call(bf16[1024,1024]{1,0:T(8,128)(2,1)S(1)} %get-tuple-element.38.put, ...), custom_call_target="tpu_custom_call" | custom-call | flops 800000000 | bytes 4000000 | tf_op jit(solution)/shard_map/pallas_call | solution.py:271
  41.2 15.2 %all_to_all.15 = f32[64,4,128]{2,1,0:T(4,128)S(1)} all-to-all(f32[64,4,128]{2,1,0:T(4,128)S(1)} %bitcast.6), channel_id=1, replica_groups=mesh['z'=12,'x'=4,'core'=2,'y'=8] {'x','core','y'}, dimensions={0} | all-to-all | bytes 262144 | tf_op jit(solution)/shard_map/all_to_all | solution.py:244
  56.5 24.8 %all_to_all.16 = f32[12,4,128]{2,1,0:T(4,128)S(1)} all-to-all(f32[12,4,128]{2,1,0:T(4,128)S(1)} %broadcast_in_dim.8), channel_id=1, replica_groups=mesh['z'=12,'x'=4,'core'=2,'y'=8] {'z'}, dimensions={0} | all-to-all | bytes 49152 | tf_op jit(solution)/shard_map/all_to_all | solution.py:246
  81.3 0.7 broadcast_in_dim.9
  82.0 8.8 %all-to-all-start.2 = ((f32[64,4,128]{2,1,0:T(4,128)}), f32[64,4,128]{2,1,0:T(4,128)S(1)}, u32[]{:S(2)}, u32[]{:S(2)}) async-start(f32[64,4,128]{2,1,0:T(4,128)} %broadcast_in_dim.9), calls=%async_computation.2 | async-start | bytes 262144 | tf_op jit(solution)/shard_map/all_to_all | solution.py:248
  90.8 2.1 %collective-permute-start.8 = (bf16[256,128]{1,0:T(8,128)(2,1)}, bf16[256,128]{1,0:T(8,128)(2,1)}, u32[]{:S(2)}, u32[]{:S(2)}) collective-permute-start(bf16[256,128]{1,0:T(8,128)(2,1)} %copy-done.3), channel_id=1, source_target_pairs={{0,8},{8,16},{16,24},{24,32},{32,40},{40,48},{48,56},{56,64},{64,7... | collective-permute-start | bytes 196616 | tf_op jit(solution)/shard_map/ppermute | solution.py:233
  92.9 5.6 %collective-permute-start.9 = (bf16[256,128]{1,0:T(8,128)(2,1)}, bf16[256,128]{1,0:T(8,128)(2,1)}, u32[]{:S(2)}, u32[]{:S(2)}) collective-permute-start(bf16[256,128]{1,0:T(8,128)(2,1)} %copy-done.2), channel_id=1, source_target_pairs={{8,0},{16,8},{24,16},{32,24},{40,32},{48,40},{56,48},{64,56},{72,6... | collective-permute-start | bytes 196616 | tf_op jit(solution)/shard_map/ppermute | solution.py:234
  98.5 2.5 %collective-permute-start.10 = (bf16[256,128]{1,0:T(8,128)(2,1)}, bf16[256,128]{1,0:T(8,128)(2,1)}, u32[]{:S(2)}, u32[]{:S(2)}) collective-permute-start(bf16[256,128]{1,0:T(8,128)(2,1)} %copy-done.1), channel_id=1, source_target_pairs={{0,1},{1,2},{2,3},{3,4},{4,5},{5,6},{6,7},{8,9},{9,10},{10,11},{11... | collective-permute-start | bytes 196616 | tf_op jit(solution)/shard_map/ppermute | solution.py:235
  101.0 4.8 %collective-permute-start.11 = (bf16[256,128]{1,0:T(8,128)(2,1)}, bf16[256,128]{1,0:T(8,128)(2,1)}, u32[]{:S(2)}, u32[]{:S(2)}) collective-permute-start(bf16[256,128]{1,0:T(8,128)(2,1)} %copy-done), channel_id=1, source_target_pairs={{1,0},{2,1},{3,2},{4,3},{5,4},{6,5},{7,6},{9,8},{10,9},{11,10},{12... | collective-permute-start | bytes 196616 | tf_op jit(solution)/shard_map/ppermute | solution.py:236
  105.8 8.1 %shard_map.101.alpha = f32[128,128]{1,0:T(8,128)S(1)} custom-call(f32[64,4,128]{2,1,0:T(4,128)S(1)} %all-to-all-done.2.both), custom_call_target="tpu_custom_call" | custom-call | flops 100000000 | bytes 4000000 | tf_op jit(solution)/shard_map/pallas_call | solution.py:286
  113.9 3.7 %shard_map.102 = (f32[1024,128]{1,0:T(8,128)}, f32[1024,128]{1,0:T(8,128)}) custom-call(bf16[1024,1024]{1,0:T(8,128)(2,1)S(1)} %get-tuple-element.38.put, bf16[256,128]{1,0:T(8,128)(2,1)} %collective-permute-done.8.r0, bf16[256,128]{1,0:T(8,128)(2,1)} %collective-permute-done.9.r1, bf16[256,128]{1,0:T(8,128)(2,1)} %collective-permute-done.10.r2, ...), custom_call_target="tpu_custom_call" | custom-call | flops 100000000 | bytes 4000000 | tf_op jit(solution)/shard_map/pallas_call | solution.py:288
  (25 shorter events, 1.1 us)
Async XLA Ops:
  2.8 16.2 %collective-permute-start = (bf16[256,128]{1,0:T(8,128)(2,1)S(1)}, bf16[256,128]{1,0:T(8,128)(2,1)S(1)}, u32[]{:S(2)}, u32[]{:S(2)}) collective-permute-start(bf16[256,128]{1,0:T(8,128)(2,1)S(1)} %get-tuple-element.46), channel_id=1, source_target_pairs={{0,8},{8,16},{16,24},{24,32},{32,40},{40,48},{48,56},{56,64},{64,7... | collective-permute-start | bytes 196616 | tf_op jit(solution)/shard_map/ppermute | solution.py:233
  4.7 14.3 %collective-permute-start.1 = (bf16[256,128]{1,0:T(8,128)(2,1)S(1)}, bf16[256,128]{1,0:T(8,128)(2,1)S(1)}, u32[]{:S(2)}, u32[]{:S(2)}) collective-permute-start(bf16[256,128]{1,0:T(8,128)(2,1)S(1)} %get-tuple-element.47), channel_id=1, source_target_pairs={{8,0},{16,8},{24,16},{32,24},{40,32},{48,40},{56,48},{64,56},{72,6... | collective-permute-start | bytes 196616 | tf_op jit(solution)/shard_map/ppermute | solution.py:234
  10.5 8.5 %collective-permute-start.2 = (bf16[256,128]{1,0:T(8,128)(2,1)S(1)}, bf16[256,128]{1,0:T(8,128)(2,1)S(1)}, u32[]{:S(2)}, u32[]{:S(2)}) collective-permute-start(bf16[256,128]{1,0:T(8,128)(2,1)S(1)} %get-tuple-element.48), channel_id=1, source_target_pairs={{0,1},{1,2},{2,3},{3,4},{4,5},{5,6},{6,7},{8,9},{9,10},{10,11},{11... | collective-permute-start | bytes 196616 | tf_op jit(solution)/shard_map/ppermute | solution.py:235
  13.1 6.4 %collective-permute-start.3 = (bf16[256,128]{1,0:T(8,128)(2,1)S(1)}, bf16[256,128]{1,0:T(8,128)(2,1)S(1)}, u32[]{:S(2)}, u32[]{:S(2)}) collective-permute-start(bf16[256,128]{1,0:T(8,128)(2,1)S(1)} %get-tuple-element.49), channel_id=1, source_target_pairs={{1,0},{2,1},{3,2},{4,3},{5,4},{6,5},{7,6},{9,8},{10,9},{11,10},{12... | collective-permute-start | bytes 196616 | tf_op jit(solution)/shard_map/ppermute | solution.py:236
  21.5 15.5 %collective-permute-start.4 = (bf16[256,128]{1,0:T(8,128)(2,1)S(1)}, bf16[256,128]{1,0:T(8,128)(2,1)S(1)}, u32[]{:S(2)}, u32[]{:S(2)}) collective-permute-start(bf16[256,128]{1,0:T(8,128)(2,1)S(1)} %get-tuple-element.51), channel_id=1, source_target_pairs={{0,8},{8,16},{16,24},{24,32},{32,40},{40,48},{48,56},{56,64},{64,7... | collective-permute-start | bytes 196616 | tf_op jit(solution)/shard_map/ppermute | solution.py:233
  23.4 13.5 %collective-permute-start.5 = (bf16[256,128]{1,0:T(8,128)(2,1)S(1)}, bf16[256,128]{1,0:T(8,128)(2,1)S(1)}, u32[]{:S(2)}, u32[]{:S(2)}) collective-permute-start(bf16[256,128]{1,0:T(8,128)(2,1)S(1)} %get-tuple-element.52), channel_id=1, source_target_pairs={{8,0},{16,8},{24,16},{32,24},{40,32},{48,40},{56,48},{64,56},{72,6... | collective-permute-start | bytes 196616 | tf_op jit(solution)/shard_map/ppermute | solution.py:234
  29.2 7.8 %collective-permute-start.6 = (bf16[256,128]{1,0:T(8,128)(2,1)S(1)}, bf16[256,128]{1,0:T(8,128)(2,1)S(1)}, u32[]{:S(2)}, u32[]{:S(2)}) collective-permute-start(bf16[256,128]{1,0:T(8,128)(2,1)S(1)} %get-tuple-element.53), channel_id=1, source_target_pairs={{0,1},{1,2},{2,3},{3,4},{4,5},{5,6},{6,7},{8,9},{9,10},{10,11},{11... | collective-permute-start | bytes 196616 | tf_op jit(solution)/shard_map/ppermute | solution.py:235
  31.6 6.9 %collective-permute-start.7 = (bf16[256,128]{1,0:T(8,128)(2,1)S(1)}, bf16[256,128]{1,0:T(8,128)(2,1)S(1)}, u32[]{:S(2)}, u32[]{:S(2)}) collective-permute-start(bf16[256,128]{1,0:T(8,128)(2,1)S(1)} %get-tuple-element.54), channel_id=1, source_target_pairs={{1,0},{2,1},{3,2},{4,3},{5,4},{6,5},{7,6},{9,8},{10,9},{11,10},{12... | collective-permute-start | bytes 196616 | tf_op jit(solution)/shard_map/ppermute | solution.py:236
  40.5 0.6 copy-start
  40.5 0.6 copy-start.1
  40.5 0.7 copy-start.2
  40.5 0.7 copy-start.3
  82.0 23.8 %all-to-all-start.2 = ((f32[64,4,128]{2,1,0:T(4,128)}), f32[64,4,128]{2,1,0:T(4,128)S(1)}, u32[]{:S(2)}, u32[]{:S(2)}) async-start(f32[64,4,128]{2,1,0:T(4,128)} %broadcast_in_dim.9), calls=%async_computation.2 | async-start | bytes 262144 | tf_op jit(solution)/shard_map/all_to_all | solution.py:248
  90.8 23.1 %collective-permute-start.8 = (bf16[256,128]{1,0:T(8,128)(2,1)}, bf16[256,128]{1,0:T(8,128)(2,1)}, u32[]{:S(2)}, u32[]{:S(2)}) collective-permute-start(bf16[256,128]{1,0:T(8,128)(2,1)} %copy-done.3), channel_id=1, source_target_pairs={{0,8},{8,16},{16,24},{24,32},{32,40},{40,48},{48,56},{56,64},{64,7... | collective-permute-start | bytes 196616 | tf_op jit(solution)/shard_map/ppermute | solution.py:233
  92.9 21.0 %collective-permute-start.9 = (bf16[256,128]{1,0:T(8,128)(2,1)}, bf16[256,128]{1,0:T(8,128)(2,1)}, u32[]{:S(2)}, u32[]{:S(2)}) collective-permute-start(bf16[256,128]{1,0:T(8,128)(2,1)} %copy-done.2), channel_id=1, source_target_pairs={{8,0},{16,8},{24,16},{32,24},{40,32},{48,40},{56,48},{64,56},{72,6... | collective-permute-start | bytes 196616 | tf_op jit(solution)/shard_map/ppermute | solution.py:234
  98.5 15.4 %collective-permute-start.10 = (bf16[256,128]{1,0:T(8,128)(2,1)}, bf16[256,128]{1,0:T(8,128)(2,1)}, u32[]{:S(2)}, u32[]{:S(2)}) collective-permute-start(bf16[256,128]{1,0:T(8,128)(2,1)} %copy-done.1), channel_id=1, source_target_pairs={{0,1},{1,2},{2,3},{3,4},{4,5},{5,6},{6,7},{8,9},{9,10},{10,11},{11... | collective-permute-start | bytes 196616 | tf_op jit(solution)/shard_map/ppermute | solution.py:235
  101.0 12.9 %collective-permute-start.11 = (bf16[256,128]{1,0:T(8,128)(2,1)}, bf16[256,128]{1,0:T(8,128)(2,1)}, u32[]{:S(2)}, u32[]{:S(2)}) collective-permute-start(bf16[256,128]{1,0:T(8,128)(2,1)} %copy-done), channel_id=1, source_target_pairs={{1,0},{2,1},{3,2},{4,3},{5,4},{6,5},{7,6},{9,8},{10,9},{11,10},{12... | collective-permute-start | bytes 196616 | tf_op jit(solution)/shard_map/ppermute | solution.py:236

commit v3 on v2

--- a/solution.py
+++ b/solution.py
@@ -6,6 +6,7 @@
 from jax.experimental import pallas as pl
 from jax.experimental.pallas import tpu as pltpu
 from jax.sharding import Mesh, PartitionSpec as P
+
 
 X_CHIPS, CORES = 4, 2
 SPAN = ("z", "x", "core")
@@ -115,7 +116,6 @@
 def apply_kernel(put, pick, block, sign_row, scale, base, r0, r1, r2, r3, partner, term, s0, s1, s2, s3, operand):
     size = put.shape[0]
     scale_cols = columns([scale[0, :, i * 128 : (i + 1) * 128] for i in range(size // 128)])
-    factors = []
     for i in range(size // TILE):
         here = slice(i * TILE, (i + 1) * TILE)
         got = None
@@ -202,8 +202,20 @@
         alpha[8 * t : 8 * t + 8, :] = g[t]
 
 
-def finish_kernel(put, r0, r1, r2, r3, gap, part0, term1, part1, term2, alpha, mult, resid, mult_v, resid_v, sems):
-    size = put.shape[0]
+def place_kernel(first, rows, r0, r1, out):
+    slots = r0.shape[0]
+    down = lax.broadcasted_iota(jnp.int32, (TILE, slots), 0)
+    for i in range(out.shape[0] // TILE):
+        got = None
+        for d, r in ((first, r0), (first + 1, r1)):
+            hit = down + i * TILE == rows[0, 0, d : d + 1, :]
+            piece = mm(jnp.where(hit, 1.0, 0.0).astype(BF), r[...])
+            got = piece if got is None else got + piece
+        out[i * TILE : (i + 1) * TILE, :] = got.astype(BF)
+
+
+def finish_kernel(gap, part0, term1, part1, term2, span2, chord2, alpha, mult, resid, mult_v, resid_v, sems):
+    size = gap.shape[0]
     pieces = split3(alpha[...])
     moves = []
     for i in range(size // TILE):
@@ -211,12 +223,7 @@
         mult_v[here, :] = sum(mm(f, p) for p in pieces[::-1] for f in (term1[here, :], part1[here, :]))
         moves.append(pltpu.make_async_copy(mult_v.at[here, :], mult.at[here, :], sems.at[0, i]))
         moves[-1].start()
-        got = None
-        for d, r in enumerate((r0, r1, r2, r3)):
-            slots = r.shape[0]
-            piece = mm(put[here, d * slots : (d + 1) * slots], r[...])
-            got = piece if got is None else got + piece
-        got = got.astype(BF)
+        got = span2[here, :] + chord2[here, :]
         step = sum(mm(f, p) for p in pieces[::-1] for f in (term2[here, :], got))
         resid_v[here, :] = gap[here, :].astype(F32) + part0[here, :].astype(F32) - step
         moves.append(pltpu.make_async_copy(resid_v.at[here, :], resid.at[here, :], sems.at[1, i]))
@@ -229,12 +236,11 @@
     span_count, chord_count = sizes
     up = lambda n: [(i, i + 1) for i in range(n - 1)]
     down = lambda n: [(i + 1, i) for i in range(n - 1)]
-    return (
-        lax.ppermute(piece[1], SPAN, up(span_count)),
-        lax.ppermute(piece[0], SPAN, down(span_count)),
-        lax.ppermute(piece[3], "y", up(chord_count)),
-        lax.ppermute(piece[2], "y", down(chord_count)),
-    )
+    a = lax.ppermute(piece[1], SPAN, up(span_count))
+    b = lax.ppermute(piece[0], SPAN, down(span_count))
+    c = lax.ppermute(piece[3], "y", up(chord_count))
+    d = lax.ppermute(piece[2], "y", down(chord_count))
+    return a, b, c, d
 
 
 def reduce_all(value):
@@ -245,8 +251,7 @@
     chunk = jnp.sum(chunks, axis=0)
     layers = lax.all_to_all(jnp.broadcast_to(chunk[None], (height,) + chunk.shape), "z", 0, 0)
     chunk = jnp.sum(layers, axis=0)
-    whole = lax.all_to_all(jnp.broadcast_to(chunk[None], (plane,) + chunk.shape), PLANE, 0, 0)
-    return whole
+    return lax.all_to_all(jnp.broadcast_to(chunk[None], (plane,) + chunk.shape), PLANE, 0, 0)
 
 
 def shards(sizes, disp, packed, fscale, dscale, diag, rows, signs, counts):
@@ -282,16 +287,18 @@
     part1, term2, sent = operate(flex, fscale, term1, got1)
     got2 = exchange(sent, sizes)
     curv = local_gram(term1, part1, term2)
+    span2 = call(functools.partial(place_kernel, 0), [field], [VM] * 3)(rows, *got2[:2])[0]
+    chord2 = call(functools.partial(place_kernel, 2), [field], [VM] * 3)(rows, *got2[2:])[0]
     both = reduce_all(jnp.concatenate([gamma, curv], axis=0))
     alpha = call(solve_kernel, [((width, width), F32)], [VM])(both)[0]
     whole = ((size, width), F32)
     mult, resid = call(
         finish_kernel,
         [whole] * 2,
-        [VM] * 11,
+        [VM] * 8,
         [pltpu.VMEM(*whole), pltpu.VMEM(*whole), pltpu.SemaphoreType.DMA((2, size // TILE))],
         out_spec=HB,
-    )(put, *got2, gap, part0, term1, part1, term2, alpha)
+    )(gap, part0, term1, part1, term2, span2, chord2, alpha)
     return mult[None, None], resid[None, None]
 
 

time: 118 us -> 121 us (1.025)
  the two profiles are of different devices: /device:TPU:96 before, /device:TPU:39 now
where the time goes in v3:
time: 121 us; the launch traced here: 120 us
  starting transfers between devices  52.7 us (44%)
  blocking collectives  40.7 us (34%)
  Pallas kernels  19.1 us (16%)
  waiting for transfers between devices  5.92 us (5%)
    all_to_all x1, blocking collectives, reduce_all(): lax.all_to_all(jnp.broadcast_to(chunk[None], (height,) + chunk.shape), 'z...  26 us
    all_to_all x1, blocking collectives, reduce_all(): lax.all_to_all(value.reshape(plane, rows // plane, width), PLANE, 0, 0)  14.7 us
    ppermute x3, starting transfers between devices, exchange(): a = lax.ppermute(piece[1], SPAN, up(span_count))  13.8 us
    ppermute x3, starting transfers between devices, exchange(): d = lax.ppermute(piece[2], 'y', down(chord_count))  13.5 us
    all_to_all x1, starting transfers between devices, reduce_all(): lax.all_to_all(jnp.broadcast_to(chunk[None], (plane,) + chunk.shape), PLA...  12.7 us
    pallas_call x1, Pallas kernels, shards(): alpha = call(solve_kernel, [((width, width), F32)], [VM])(both)[0]  8.09 us
    ppermute x3, starting transfers between devices, exchange(): c = lax.ppermute(piece[3], 'y', up(chord_count))  6.62 us
    ppermute x3, starting transfers between devices, exchange(): b = lax.ppermute(piece[0], SPAN, down(span_count))  6.1 us
  transfers between devices with their start and end apart: 13, of which 2 were waited for; matrix products, arithmetic and copies ran while one was open for 0% of the time, Pallas kernels for 2%

profile of v3, /device:TPU:39, one launch (start us, length us, event | category | flops | bytes accessed | tf_op | source)
XLA Modules:
  0.0 120.2 jit_solution(10576438994148139104)
XLA Ops:
  0.6 2.2 %shard_map.95 = (bf16[1024,1024]{1,0:T(8,128)(2,1)S(1)}, bf16[256,128]{1,0:T(8,128)(2,1)S(1)}, bf16[256,128]{1,0:T(8,128)(2,1)S(1)}, bf16[256,128]{1,0:T(8,128)(...) custom-call(s32[1,1,4,256]{3,2,1,0:T(4,128)} %rows.1, ...), custom_call_target="tpu_custom_call" | custom-call | flops 100000000 | bytes 4000000 | tf_op jit(solution)/shard_map/pallas_call | solution.py:263
  2.8 4.5 %collective-permute-start = (bf16[256,128]{1,0:T(8,128)(2,1)S(1)}, bf16[256,128]{1,0:T(8,128)(2,1)S(1)}, u32[]{:S(2)}, u32[]{:S(2)}) collective-permute-start(bf16[256,128]{1,0:T(8,128)(2,1)S(1)} %get-tuple-element.44), channel_id=1, source_target_pairs={{0,8},{8,16},{16,24},{24,32},{32,40},{40,48},{48,56},{56,64},{64,7... | collective-permute-start | bytes 196616 | tf_op jit(solution)/shard_map/ppermute | solution.py:239
  7.3 1.9 %collective-permute-start.1 = (bf16[256,128]{1,0:T(8,128)(2,1)S(1)}, bf16[256,128]{1,0:T(8,128)(2,1)S(1)}, u32[]{:S(2)}, u32[]{:S(2)}) collective-permute-start(bf16[256,128]{1,0:T(8,128)(2,1)S(1)} %get-tuple-element.45), channel_id=1, source_target_pairs={{8,0},{16,8},{24,16},{32,24},{40,32},{48,40},{56,48},{64,56},{72,6... | collective-permute-start | bytes 196616 | tf_op jit(solution)/shard_map/ppermute | solution.py:240
  9.2 2.3 %collective-permute-start.2 = (bf16[256,128]{1,0:T(8,128)(2,1)S(1)}, bf16[256,128]{1,0:T(8,128)(2,1)S(1)}, u32[]{:S(2)}, u32[]{:S(2)}) collective-permute-start(bf16[256,128]{1,0:T(8,128)(2,1)S(1)} %get-tuple-element.46), channel_id=1, source_target_pairs={{0,1},{1,2},{2,3},{3,4},{4,5},{5,6},{6,7},{8,9},{9,10},{10,11},{11... | collective-permute-start | bytes 196616 | tf_op jit(solution)/shard_map/ppermute | solution.py:241
  11.6 4.2 %collective-permute-start.3 = (bf16[256,128]{1,0:T(8,128)(2,1)S(1)}, bf16[256,128]{1,0:T(8,128)(2,1)S(1)}, u32[]{:S(2)}, u32[]{:S(2)}) collective-permute-start(bf16[256,128]{1,0:T(8,128)(2,1)S(1)} %get-tuple-element.47), channel_id=1, source_target_pairs={{1,0},{2,1},{3,2},{4,3},{5,4},{6,5},{7,6},{9,8},{10,9},{11,10},{12... | collective-permute-start | bytes 196616 | tf_op jit(solution)/shard_map/ppermute | solution.py:242
  15.8 1.4 %shard_map.96 = (bf16[1024,1024]{1,0:T(8,128)(2,1)S(1)}, bf16[1024,128]{1,0:T(8,128)(2,1)S(1)}, bf16[1024,128]{1,0:T(8,128)(2,1)S(1)}, bf16[1024,1024]{1,0:T(8,128)(2,1)S(1)}, bf16[1024,1024]{1,0:T(8,128)(2,1)S(1)}) custom-call(s32[1,1,4,256]{3,2,1,0:T(4,128)S(1)} %get-tuple-element.33.rows, bf16[1024,128]{1,0:T(8,128)(2,1)S(1)} %get-tuple-element.34.live_sign, ...), custom_call_target="tpu_custom_call" | custom-call | flops 100000000 | bytes 4000000 | tf_op jit(solution)/shard_map/pallas_call | solution.py:271
  17.2 2.1 %shard_map.97 = (bf16[1024,128]{1,0:T(8,128)(2,1)S(1)}, bf16[1024,128]{1,0:T(8,128)(2,1)S(1)}, bf16[256,128]{1,0:T(8,128)(2,1)S(1)}, bf16[256,128]{1,0:T(8,128)(...) custom-call(bf16[1024,1024]{1,0:T(8,128)(2,1)S(1)} %get-tuple-element.39.put, ...), custom_call_target="tpu_custom_call" | custom-call | flops 800000000 | bytes 4000000 | tf_op jit(solution)/shard_map/pallas_call | solution.py:276
  19.3 6.7 %collective-permute-start.4 = (bf16[256,128]{1,0:T(8,128)(2,1)S(1)}, bf16[256,128]{1,0:T(8,128)(2,1)S(1)}, u32[]{:S(2)}, u32[]{:S(2)}) collective-permute-start(bf16[256,128]{1,0:T(8,128)(2,1)S(1)} %get-tuple-element.52), channel_id=1, source_target_pairs={{0,8},{8,16},{16,24},{24,32},{32,40},{40,48},{48,56},{56,64},{64,7... | collective-permute-start | bytes 196616 | tf_op jit(solution)/shard_map/ppermute | solution.py:239
  26.0 1.9 %collective-permute-start.5 = (bf16[256,128]{1,0:T(8,128)(2,1)S(1)}, bf16[256,128]{1,0:T(8,128)(2,1)S(1)}, u32[]{:S(2)}, u32[]{:S(2)}) collective-permute-start(bf16[256,128]{1,0:T(8,128)(2,1)S(1)} %get-tuple-element.53), channel_id=1, source_target_pairs={{8,0},{16,8},{24,16},{32,24},{40,32},{48,40},{56,48},{64,56},{72,6... | collective-permute-start | bytes 196616 | tf_op jit(solution)/shard_map/ppermute | solution.py:240
  27.9 2.1 %collective-permute-start.6 = (bf16[256,128]{1,0:T(8,128)(2,1)S(1)}, bf16[256,128]{1,0:T(8,128)(2,1)S(1)}, u32[]{:S(2)}, u32[]{:S(2)}) collective-permute-start(bf16[256,128]{1,0:T(8,128)(2,1)S(1)} %get-tuple-element.54), channel_id=1, source_target_pairs={{0,1},{1,2},{2,3},{3,4},{4,5},{5,6},{6,7},{8,9},{9,10},{10,11},{11... | collective-permute-start | bytes 196616 | tf_op jit(solution)/shard_map/ppermute | solution.py:241
  30.1 5.0 %collective-permute-start.7 = (bf16[256,128]{1,0:T(8,128)(2,1)S(1)}, bf16[256,128]{1,0:T(8,128)(2,1)S(1)}, u32[]{:S(2)}, u32[]{:S(2)}) collective-permute-start(bf16[256,128]{1,0:T(8,128)(2,1)S(1)} %get-tuple-element.55), channel_id=1, source_target_pairs={{1,0},{2,1},{3,2},{4,3},{5,4},{6,5},{7,6},{9,8},{10,9},{11,10},{12... | collective-permute-start | bytes 196616 | tf_op jit(solution)/shard_map/ppermute | solution.py:242
  35.4 0.9 collective-permute-done.7.r3
  36.4 2.0 %shard_map.98 = (bf16[1024,128]{1,0:T(8,128)(2,1)S(1)}, bf16[1024,128]{1,0:T(8,128)(2,1)S(1)}, bf16[256,128]{1,0:T(8,128)(2,1)S(1)}, bf16[256,128]{1,0:T(8,128)(...) custom-call(bf16[1024,1024]{1,0:T(8,128)(2,1)S(1)} %get-tuple-element.39.put, ...), custom_call_target="tpu_custom_call" | custom-call | flops 800000000 | bytes 4000000 | tf_op jit(solution)/shard_map/pallas_call | solution.py:276
  38.8 14.7 %all_to_all.15 = f32[64,4,128]{2,1,0:T(4,128)S(1)} all-to-all(f32[64,4,128]{2,1,0:T(4,128)S(1)} %bitcast.6), channel_id=1, replica_groups=mesh['z'=12,'x'=4,'core'=2,'y'=8] {'x','core','y'}, dimensions={0} | all-to-all | bytes 262144 | tf_op jit(solution)/shard_map/all_to_all | solution.py:250
  53.6 26.0 %all_to_all.16 = f32[12,4,128]{2,1,0:T(4,128)S(1)} all-to-all(f32[12,4,128]{2,1,0:T(4,128)S(1)} %broadcast_in_dim.8), channel_id=1, replica_groups=mesh['z'=12,'x'=4,'core'=2,'y'=8] {'z'}, dimensions={0} | all-to-all | bytes 49152 | tf_op jit(solution)/shard_map/all_to_all | solution.py:252
  79.6 0.7 broadcast_in_dim.9
  80.3 12.7 %all-to-all-start.2 = ((f32[64,4,128]{2,1,0:T(4,128)}), f32[64,4,128]{2,1,0:T(4,128)S(1)}, u32[]{:S(2)}, u32[]{:S(2)}) async-start(f32[64,4,128]{2,1,0:T(4,128)} %broadcast_in_dim.9), calls=%async_computation.2 | async-start | bytes 262144 | tf_op jit(solution)/shard_map/all_to_all | solution.py:254
  92.9 2.2 %collective-permute-start.10 = (bf16[256,128]{1,0:T(8,128)(2,1)S(1)}, bf16[256,128]{1,0:T(8,128)(2,1)S(1)}, u32[]{:S(2)}, u32[]{:S(2)}) collective-permute-start(bf16[256,128]{1,0:T(8,128)(2,1)S(1)} %get-tuple-element.60), channel_id=1, source_target_pairs={{0,1},{1,2},{2,3},{3,4},{4,5},{5,6},{6,7},{8,9},{9,10},{10,11},{11... | collective-permute-start | bytes 196616 | tf_op jit(solution)/shard_map/ppermute | solution.py:241
  95.1 4.3 %collective-permute-start.11 = (bf16[256,128]{1,0:T(8,128)(2,1)S(1)}, bf16[256,128]{1,0:T(8,128)(2,1)S(1)}, u32[]{:S(2)}, u32[]{:S(2)}) collective-permute-start(bf16[256,128]{1,0:T(8,128)(2,1)S(1)} %get-tuple-element.61), channel_id=1, source_target_pairs={{1,0},{2,1},{3,2},{4,3},{5,4},{6,5},{7,6},{9,8},{10,9},{11,10},{12... | collective-permute-start | bytes 196616 | tf_op jit(solution)/shard_map/ppermute | solution.py:242
  99.4 2.6 %collective-permute-start.8 = (bf16[256,128]{1,0:T(8,128)(2,1)S(1)}, bf16[256,128]{1,0:T(8,128)(2,1)S(1)}, u32[]{:S(2)}, u32[]{:S(2)}) collective-permute-start(bf16[256,128]{1,0:T(8,128)(2,1)S(1)} %get-tuple-element.58), channel_id=1, source_target_pairs={{0,8},{8,16},{16,24},{24,32},{32,40},{40,48},{48,56},{56,64},{64,7... | collective-permute-start | bytes 196616 | tf_op jit(solution)/shard_map/ppermute | solution.py:239
  102.1 2.3 %collective-permute-start.9 = (bf16[256,128]{1,0:T(8,128)(2,1)S(1)}, bf16[256,128]{1,0:T(8,128)(2,1)S(1)}, u32[]{:S(2)}, u32[]{:S(2)}) collective-permute-start(bf16[256,128]{1,0:T(8,128)(2,1)S(1)} %get-tuple-element.59), channel_id=1, source_target_pairs={{8,0},{16,8},{24,16},{32,24},{40,32},{48,40},{56,48},{64,56},{72,6... | collective-permute-start | bytes 196616 | tf_op jit(solution)/shard_map/ppermute | solution.py:240
  104.8 5.0 %collective-permute-done.9.r1 = bf16[256,128]{1,0:T(8,128)(2,1)S(1)} collective-permute-done((bf16[256,128]{1,0:T(8,128)(2,1)S(1)}, bf16[256,128]{1,0:T(8,128)(2,1)S(1)}, u32[]{:S(2)}, u32[]{:S(2)}) %collective-permute-start.9) | collective-permute-done | bytes 65568 | tf_op jit(solution)/shard_map/ppermute | solution.py:240
  110.2 8.1 %shard_map.103.alpha = f32[128,128]{1,0:T(8,128)S(1)} custom-call(f32[64,4,128]{2,1,0:T(4,128)S(1)} %all-to-all-done.2.both), custom_call_target="tpu_custom_call" | custom-call | flops 100000000 | bytes 4000000 | tf_op jit(solution)/shard_map/pallas_call | solution.py:293
  118.3 1.7 %shard_map.104 = (f32[1024,128]{1,0:T(8,128)}, f32[1024,128]{1,0:T(8,128)}) custom-call(bf16[1024,128]{1,0:T(8,128)(2,1)S(1)} %get-tuple-element.38.base.gap, bf16[1024,128]{1,0:T(8,128)(2,1)S(1)} %get-tuple-element.48.partner.part0, bf16[1024,128]{1,0:T(8,128)(2,1)S(1)} %get-tuple-element.49.base.term.term1, ...), custom_call_target="tpu_custom_call" | custom-call | flops 100000000 | bytes 4000000 | tf_op jit(solution)/shard_map/pallas_call | solution.py:295
  (19 shorter events, 1.7 us)
Async XLA Ops:
  2.8 14.3 %collective-permute-start = (bf16[256,128]{1,0:T(8,128)(2,1)S(1)}, bf16[256,128]{1,0:T(8,128)(2,1)S(1)}, u32[]{:S(2)}, u32[]{:S(2)}) collective-permute-start(bf16[256,128]{1,0:T(8,128)(2,1)S(1)} %get-tuple-element.44), channel_id=1, source_target_pairs={{0,8},{8,16},{16,24},{24,32},{32,40},{40,48},{48,56},{56,64},{64,7... | collective-permute-start | bytes 196616 | tf_op jit(solution)/shard_map/ppermute | solution.py:239
  7.3 9.9 %collective-permute-start.1 = (bf16[256,128]{1,0:T(8,128)(2,1)S(1)}, bf16[256,128]{1,0:T(8,128)(2,1)S(1)}, u32[]{:S(2)}, u32[]{:S(2)}) collective-permute-start(bf16[256,128]{1,0:T(8,128)(2,1)S(1)} %get-tuple-element.45), channel_id=1, source_target_pairs={{8,0},{16,8},{24,16},{32,24},{40,32},{48,40},{56,48},{64,56},{72,6... | collective-permute-start | bytes 196616 | tf_op jit(solution)/shard_map/ppermute | solution.py:240
  9.2 8.0 %collective-permute-start.2 = (bf16[256,128]{1,0:T(8,128)(2,1)S(1)}, bf16[256,128]{1,0:T(8,128)(2,1)S(1)}, u32[]{:S(2)}, u32[]{:S(2)}) collective-permute-start(bf16[256,128]{1,0:T(8,128)(2,1)S(1)} %get-tuple-element.46), channel_id=1, source_target_pairs={{0,1},{1,2},{2,3},{3,4},{4,5},{5,6},{6,7},{8,9},{9,10},{10,11},{11... | collective-permute-start | bytes 196616 | tf_op jit(solution)/shard_map/ppermute | solution.py:241
  11.6 5.7 %collective-permute-start.3 = (bf16[256,128]{1,0:T(8,128)(2,1)S(1)}, bf16[256,128]{1,0:T(8,128)(2,1)S(1)}, u32[]{:S(2)}, u32[]{:S(2)}) collective-permute-start(bf16[256,128]{1,0:T(8,128)(2,1)S(1)} %get-tuple-element.47), channel_id=1, source_target_pairs={{1,0},{2,1},{3,2},{4,3},{5,4},{6,5},{7,6},{9,8},{10,9},{11,10},{12... | collective-permute-start | bytes 196616 | tf_op jit(solution)/shard_map/ppermute | solution.py:242
  19.3 16.1 %collective-permute-start.4 = (bf16[256,128]{1,0:T(8,128)(2,1)S(1)}, bf16[256,128]{1,0:T(8,128)(2,1)S(1)}, u32[]{:S(2)}, u32[]{:S(2)}) collective-permute-start(bf16[256,128]{1,0:T(8,128)(2,1)S(1)} %get-tuple-element.52), channel_id=1, source_target_pairs={{0,8},{8,16},{16,24},{24,32},{32,40},{40,48},{48,56},{56,64},{64,7... | collective-permute-start | bytes 196616 | tf_op jit(solution)/shard_map/ppermute | solution.py:239
  26.0 9.4 %collective-permute-start.5 = (bf16[256,128]{1,0:T(8,128)(2,1)S(1)}, bf16[256,128]{1,0:T(8,128)(2,1)S(1)}, u32[]{:S(2)}, u32[]{:S(2)}) collective-permute-start(bf16[256,128]{1,0:T(8,128)(2,1)S(1)} %get-tuple-element.53), channel_id=1, source_target_pairs={{8,0},{16,8},{24,16},{32,24},{40,32},{48,40},{56,48},{64,56},{72,6... | collective-permute-start | bytes 196616 | tf_op jit(solution)/shard_map/ppermute | solution.py:240
  27.9 7.5 %collective-permute-start.6 = (bf16[256,128]{1,0:T(8,128)(2,1)S(1)}, bf16[256,128]{1,0:T(8,128)(2,1)S(1)}, u32[]{:S(2)}, u32[]{:S(2)}) collective-permute-start(bf16[256,128]{1,0:T(8,128)(2,1)S(1)} %get-tuple-element.54), channel_id=1, source_target_pairs={{0,1},{1,2},{2,3},{3,4},{4,5},{5,6},{6,7},{8,9},{9,10},{10,11},{11... | collective-permute-start | bytes 196616 | tf_op jit(solution)/shard_map/ppermute | solution.py:241
  30.1 6.3 %collective-permute-start.7 = (bf16[256,128]{1,0:T(8,128)(2,1)S(1)}, bf16[256,128]{1,0:T(8,128)(2,1)S(1)}, u32[]{:S(2)}, u32[]{:S(2)}) collective-permute-start(bf16[256,128]{1,0:T(8,128)(2,1)S(1)} %get-tuple-element.55), channel_id=1, source_target_pairs={{1,0},{2,1},{3,2},{4,3},{5,4},{6,5},{7,6},{9,8},{10,9},{11,10},{12... | collective-permute-start | bytes 196616 | tf_op jit(solution)/shard_map/ppermute | solution.py:242
  80.3 30.0 %all-to-all-start.2 = ((f32[64,4,128]{2,1,0:T(4,128)}), f32[64,4,128]{2,1,0:T(4,128)S(1)}, u32[]{:S(2)}, u32[]{:S(2)}) async-start(f32[64,4,128]{2,1,0:T(4,128)} %broadcast_in_dim.9), calls=%async_computation.2 | async-start | bytes 262144 | tf_op jit(solution)/shard_map/all_to_all | solution.py:254
  92.9 11.4 %collective-permute-start.10 = (bf16[256,128]{1,0:T(8,128)(2,1)S(1)}, bf16[256,128]{1,0:T(8,128)(2,1)S(1)}, u32[]{:S(2)}, u32[]{:S(2)}) collective-permute-start(bf16[256,128]{1,0:T(8,128)(2,1)S(1)} %get-tuple-element.60), channel_id=1, source_target_pairs={{0,1},{1,2},{2,3},{3,4},{4,5},{5,6},{6,7},{8,9},{9,10},{10,11},{11... | collective-permute-start | bytes 196616 | tf_op jit(solution)/shard_map/ppermute | solution.py:241
  95.1 9.2 %collective-permute-start.11 = (bf16[256,128]{1,0:T(8,128)(2,1)S(1)}, bf16[256,128]{1,0:T(8,128)(2,1)S(1)}, u32[]{:S(2)}, u32[]{:S(2)}) collective-permute-start(bf16[256,128]{1,0:T(8,128)(2,1)S(1)} %get-tuple-element.61), channel_id=1, source_target_pairs={{1,0},{2,1},{3,2},{4,3},{5,4},{6,5},{7,6},{9,8},{10,9},{11,10},{12... | collective-permute-start | bytes 196616 | tf_op jit(solution)/shard_map/ppermute | solution.py:242
  99.4 5.4 %collective-permute-start.8 = (bf16[256,128]{1,0:T(8,128)(2,1)S(1)}, bf16[256,128]{1,0:T(8,128)(2,1)S(1)}, u32[]{:S(2)}, u32[]{:S(2)}) collective-permute-start(bf16[256,128]{1,0:T(8,128)(2,1)S(1)} %get-tuple-element.58), channel_id=1, source_target_pairs={{0,8},{8,16},{16,24},{24,32},{32,40},{40,48},{48,56},{56,64},{64,7... | collective-permute-start | bytes 196616 | tf_op jit(solution)/shard_map/ppermute | solution.py:239
  102.1 7.7 %collective-permute-start.9 = (bf16[256,128]{1,0:T(8,128)(2,1)S(1)}, bf16[256,128]{1,0:T(8,128)(2,1)S(1)}, u32[]{:S(2)}, u32[]{:S(2)}) collective-permute-start(bf16[256,128]{1,0:T(8,128)(2,1)S(1)} %get-tuple-element.59), channel_id=1, source_target_pairs={{8,0},{16,8},{24,16},{32,24},{40,32},{48,40},{56,48},{64,56},{72,6... | collective-permute-start | bytes 196616 | tf_op jit(solution)/shard_map/ppermute | solution.py:240

commit v4 on v2

--- a/solution.py
+++ b/solution.py
@@ -1,4 +1,5 @@
 import functools
+import operator
 
 import jax
 import jax.numpy as jnp
@@ -13,7 +14,7 @@
 
 BF, F32 = jnp.bfloat16, jnp.float32
 TILE = 256
-STEP = 4
+STEP, GROUP = 4, 8
 VM = pl.BlockSpec(memory_space=pltpu.VMEM)
 HB = pl.BlockSpec(memory_space=pltpu.HBM)
 
@@ -150,25 +151,39 @@
     return high, mid, (rest - mid.astype(F32)).astype(BF)
 
 
-def small_solve(p, r):
-    n = len(p)
-    if n == 2:
-        scale = 1.0 / (p[0][0] * p[1][1] - p[0][1] * p[1][0])
-        return [
-            (p[1][1] * scale) * r[0] - (p[0][1] * scale) * r[1],
-            (p[0][0] * scale) * r[1] - (p[1][0] * scale) * r[0],
-        ]
-    h = n // 2
-    one, rest = range(h), range(h, n)
-    a = [row[:h] for row in p[:h]]
-    across = [small_solve(a, [p[i][j] for i in one]) for j in rest]
-    u = small_solve(a, r[:h])
-    schur = [[p[i][h + j] - sum(p[i][k] * across[j][k] for k in one) for j in range(n - h)] for i in rest]
-    v = small_solve(schur, [r[i] - sum(p[i][k] * u[k] for k in one) for i in rest])
-    return [u[i] - sum(across[j][i] * v[j] for j in range(n - h)) for i in one] + v
-
-
-def solve_kernel(both, alpha):
+def total(left, right):
+    return functools.reduce(operator.add, [x * y for x, y in zip(left, right)])
+
+
+def invert2(m):
+    scale = 1.0 / (m[0][0] * m[1][1] - m[0][1] * m[1][0])
+    return [[m[1][1] * scale, -(m[0][1] * scale)], [-(m[1][0] * scale), m[0][0] * scale]]
+
+
+def times2(x, y):
+    return [[x[i][0] * y[0][j] + x[i][1] * y[1][j] for j in range(2)] for i in range(2)]
+
+
+def factor4(p):
+    block = lambda i, j: [[p[2 * i + r][2 * j + c] for c in range(2)] for r in range(2)]
+    corner = invert2(block(0, 0))
+    down = times2(block(1, 0), corner)
+    across = times2(corner, block(0, 1))
+    used = times2(block(1, 0), across)
+    rest = block(1, 1)
+    schur = invert2([[rest[i][j] - used[i][j] for j in range(2)] for i in range(2)])
+    return corner, across, down, schur
+
+
+def solve4(factors, r):
+    corner, across, down, schur = factors
+    left = [r[2 + i] - total(down[i], r[:2]) for i in range(2)]
+    high = [total(corner[i], r[:2]) for i in range(2)]
+    low = [total(schur[i], left) for i in range(2)]
+    return [high[i] - total(across[i], low) for i in range(2)] + low
+
+
+def solve_kernel(both, alpha, a_ref):
     width = alpha.shape[0]
     count = width // 8
     rows = both.shape[1]
@@ -178,33 +193,51 @@
             return both[t * 8 // rows, t * 8 % rows : t * 8 % rows + 8]
         return jnp.concatenate([both[t * (8 // rows) + k] for k in range(8 // rows)], axis=0)
 
-    g = [tile(t) for t in range(count)]
+    for t in range(count):
+        alpha[8 * t : 8 * t + 8, :] = tile(t)
     curv = jnp.concatenate([tile(count + t) for t in range(count)], axis=0)
-    curv = (curv + curv.T) * 0.5
-    a = [curv[8 * t : 8 * t + 8, :] for t in range(count)]
+    a_ref[...] = (curv + curv.T) * 0.5
     spot = lax.broadcasted_iota(jnp.int32, (8, width), 0)
+    part = lambda ref, t: ref[8 * t : 8 * t + 8, :]
+    wide = lambda x, k: jnp.broadcast_to(x[:, k : k + 1], (8, width))
     for j in range(0, width, STEP):
-        cols = [[jnp.broadcast_to(a[t][:, j + k : j + k + 1], (8, width)) for k in range(STEP)] for t in range(count)]
-        own, r0 = j // 8, j % 8
-        row = lambda x, k: jnp.broadcast_to(x[r0 + k : r0 + k + 1, :], (8, width))
-        p = [[row(cols[own][l], k) for l in range(STEP)] for k in range(STEP)]
-        na = small_solve(p, [row(a[own], k) for k in range(STEP)])
-        ng = small_solve(p, [row(g[own], k) for k in range(STEP)])
-        for t in range(count):
-            ua = a[t] - sum(cols[t][k] * na[k] for k in range(STEP))
-            ug = g[t] - sum(cols[t][k] * ng[k] for k in range(STEP))
+        own, first = j // 8, j % 8
+        row = lambda x, k: jnp.broadcast_to(x[first + k : first + k + 1, :], (8, width))
+        a_own, g_own = part(a_ref, own), part(alpha, own)
+        own_cols = [wide(a_own, j + k) for k in range(STEP)]
+        factors = factor4([[row(own_cols[l], k) for l in range(STEP)] for k in range(STEP)])
+        na = solve4(factors, [row(a_own, k) for k in range(STEP)])
+        ng = solve4(factors, [row(g_own, k) for k in range(STEP)])
+
+        def update(t, cols):
+            ua = part(a_ref, t) - total(cols, na)
+            ug = part(alpha, t) - total(cols, ng)
             if t == own:
                 for k in range(STEP):
-                    ua = jnp.where(spot == r0 + k, na[k], ua)
-                    ug = jnp.where(spot == r0 + k, ng[k], ug)
-            a[t], g[t] = ua, ug
-    for t in range(count):
-        alpha[8 * t : 8 * t + 8, :] = g[t]
-
-
-def finish_kernel(put, r0, r1, r2, r3, gap, part0, term1, part1, term2, alpha, mult, resid, mult_v, resid_v, sems):
-    size = put.shape[0]
+                    ua = jnp.where(spot == first + k, na[k], ua)
+                    ug = jnp.where(spot == first + k, ng[k], ug)
+            a_ref[8 * t : 8 * t + 8, :] = ua
+            alpha[8 * t : 8 * t + 8, :] = ug
+
+        ahead = (j + STEP) // 8
+        early = [ahead] if ahead < count and ahead != own else []
+        for t in early:
+            update(t, [wide(part(a_ref, t), j + k) for k in range(STEP)])
+        update(own, own_cols)
+        others = [t for t in range(count) if t != own and t not in early]
+        for g in range(0, len(others), GROUP):
+            chosen = others[g : g + GROUP]
+            cols = [[wide(part(a_ref, t), j + k) for t in chosen] for k in range(STEP)]
+            for q, t in enumerate(chosen):
+                update(t, [cols[k][q] for k in range(STEP)])
+
+
+def finish_kernel(
+    rows, r0, r1, r2, r3, gap, part0, term1, part1, term2, alpha, mult, resid, mult_v, resid_v, sems
+):
+    size = gap.shape[0]
     pieces = split3(alpha[...])
+    down = lax.broadcasted_iota(jnp.int32, (TILE, r0.shape[0]), 0)
     moves = []
     for i in range(size // TILE):
         here = slice(i * TILE, (i + 1) * TILE)
@@ -213,8 +246,8 @@
         moves[-1].start()
         got = None
         for d, r in enumerate((r0, r1, r2, r3)):
-            slots = r.shape[0]
-            piece = mm(put[here, d * slots : (d + 1) * slots], r[...])
+            hit = down + i * TILE == rows[0, 0, d : d + 1, :]
+            piece = mm(jnp.where(hit, 1.0, 0.0).astype(BF), r[...])
             got = piece if got is None else got + piece
         got = got.astype(BF)
         step = sum(mm(f, p) for p in pieces[::-1] for f in (term2[here, :], got))
@@ -245,8 +278,7 @@
     chunk = jnp.sum(chunks, axis=0)
     layers = lax.all_to_all(jnp.broadcast_to(chunk[None], (height,) + chunk.shape), "z", 0, 0)
     chunk = jnp.sum(layers, axis=0)
-    whole = lax.all_to_all(jnp.broadcast_to(chunk[None], (plane,) + chunk.shape), PLANE, 0, 0)
-    return whole
+    return lax.all_to_all(jnp.broadcast_to(chunk[None], (plane,) + chunk.shape), PLANE, 0, 0)
 
 
 def shards(sizes, disp, packed, fscale, dscale, diag, rows, signs, counts):
@@ -283,7 +315,7 @@
     got2 = exchange(sent, sizes)
     curv = local_gram(term1, part1, term2)
     both = reduce_all(jnp.concatenate([gamma, curv], axis=0))
-    alpha = call(solve_kernel, [((width, width), F32)], [VM])(both)[0]
+    alpha = call(solve_kernel, [((width, width), F32)], [VM], [pltpu.VMEM((width, width), F32)])(both)[0]
     whole = ((size, width), F32)
     mult, resid = call(
         finish_kernel,
@@ -291,7 +323,7 @@
         [VM] * 11,
         [pltpu.VMEM(*whole), pltpu.VMEM(*whole), pltpu.SemaphoreType.DMA((2, size // TILE))],
         out_spec=HB,
-    )(put, *got2, gap, part0, term1, part1, term2, alpha)
+    )(rows, *got2, gap, part0, term1, part1, term2, alpha)
     return mult[None, None], resid[None, None]
 
 

time: 118 us -> 115 us (0.975)
  Pallas kernels: 20.1 us -> 16.7 us
    pallas_call x1, Pallas kernels: 8.09 us -> 5.57 us  [shards(): call(solve_kernel, [((width, width), F32)], [VM], [pltpu.VMEM((width, wid...]
  transfers between devices with their start and end apart: 13 -> 13, of which waited for: 2 -> 2; matrix products, arithmetic and copies ran while one was open for 0% -> 0% of each run, Pallas kernels for 8% -> 6%
where the time goes in v4:
time: 115 us; the launch traced here: 114 us
  starting transfers between devices  53.5 us (47%)
  blocking collectives  40 us (35%)
  Pallas kernels  16.7 us (15%)
  waiting for transfers between devices  1.96 us (2%)
    all_to_all x1, blocking collectives, reduce_all(): lax.all_to_all(jnp.broadcast_to(chunk[None], (height,) + chunk.shape), 'z...  24.8 us
    ppermute x3, starting transfers between devices, exchange(): lax.ppermute(piece[0], SPAN, down(span_count))  17.1 us
    all_to_all x1, blocking collectives, reduce_all(): lax.all_to_all(value.reshape(plane, rows // plane, width), PLANE, 0, 0)  15.2 us
    ppermute x3, starting transfers between devices, exchange(): lax.ppermute(piece[2], 'y', down(chord_count))  14.2 us
    all_to_all x1, starting transfers between devices, reduce_all(): lax.all_to_all(jnp.broadcast_to(chunk[None], (plane,) + chunk.shape), PLA...  8.83 us
    ppermute x3, starting transfers between devices, exchange(): lax.ppermute(piece[3], 'y', up(chord_count))  7.46 us
    ppermute x3, starting transfers between devices, exchange(): lax.ppermute(piece[1], SPAN, up(span_count))  5.92 us
    pallas_call x1, Pallas kernels, shards(): call(solve_kernel, [((width, width), F32)], [VM], [pltpu.VMEM((width, wid...  5.57 us
  transfers between devices with their start and end apart: 13, of which 2 were waited for; matrix products, arithmetic and copies ran while one was open for 0% of the time, Pallas kernels for 6%

profile of v4, /device:TPU:96, one launch (start us, length us, event | category | flops | bytes accessed | tf_op | source)
XLA Modules:
  0.0 114.0 jit_solution(7785142804061718155)
XLA Ops:
  0.6 2.2 %shard_map.95 = (bf16[1024,1024]{1,0:T(8,128)(2,1)S(1)}, bf16[256,128]{1,0:T(8,128)(2,1)S(1)}, bf16[256,128]{1,0:T(8,128)(2,1)S(1)}, bf16[256,128]{1,0:T(8,128)(...) custom-call(s32[1,1,4,256]{3,2,1,0:T(4,128)} %rows.1, ...), custom_call_target="tpu_custom_call" | custom-call | flops 100000000 | bytes 4000000 | tf_op jit(solution)/shard_map/pallas_call | solution.py:290
  2.8 1.9 %collective-permute-start = (bf16[256,128]{1,0:T(8,128)(2,1)S(1)}, bf16[256,128]{1,0:T(8,128)(2,1)S(1)}, u32[]{:S(2)}, u32[]{:S(2)}) collective-permute-start(bf16[256,128]{1,0:T(8,128)(2,1)S(1)} %get-tuple-element.46), channel_id=1, source_target_pairs={{0,8},{8,16},{16,24},{24,32},{32,40},{40,48},{48,56},{56,64},{64,7... | collective-permute-start | bytes 196616 | tf_op jit(solution)/shard_map/ppermute | solution.py:266
  4.8 5.8 %collective-permute-start.1 = (bf16[256,128]{1,0:T(8,128)(2,1)S(1)}, bf16[256,128]{1,0:T(8,128)(2,1)S(1)}, u32[]{:S(2)}, u32[]{:S(2)}) collective-permute-start(bf16[256,128]{1,0:T(8,128)(2,1)S(1)} %get-tuple-element.47), channel_id=1, source_target_pairs={{8,0},{16,8},{24,16},{32,24},{40,32},{48,40},{56,48},{64,56},{72,6... | collective-permute-start | bytes 196616 | tf_op jit(solution)/shard_map/ppermute | solution.py:267
  10.5 2.6 %collective-permute-start.2 = (bf16[256,128]{1,0:T(8,128)(2,1)S(1)}, bf16[256,128]{1,0:T(8,128)(2,1)S(1)}, u32[]{:S(2)}, u32[]{:S(2)}) collective-permute-start(bf16[256,128]{1,0:T(8,128)(2,1)S(1)} %get-tuple-element.48), channel_id=1, source_target_pairs={{0,1},{1,2},{2,3},{3,4},{4,5},{5,6},{6,7},{8,9},{9,10},{10,11},{11... | collective-permute-start | bytes 196616 | tf_op jit(solution)/shard_map/ppermute | solution.py:268
  13.1 4.5 %collective-permute-start.3 = (bf16[256,128]{1,0:T(8,128)(2,1)S(1)}, bf16[256,128]{1,0:T(8,128)(2,1)S(1)}, u32[]{:S(2)}, u32[]{:S(2)}) collective-permute-start(bf16[256,128]{1,0:T(8,128)(2,1)S(1)} %get-tuple-element.49), channel_id=1, source_target_pairs={{1,0},{2,1},{3,2},{4,3},{5,4},{6,5},{7,6},{9,8},{10,9},{11,10},{12... | collective-permute-start | bytes 196616 | tf_op jit(solution)/shard_map/ppermute | solution.py:269
  17.6 1.4 %shard_map.96 = (bf16[1024,1024]{1,0:T(8,128)(2,1)S(1)}, bf16[1024,128]{1,0:T(8,128)(2,1)S(1)}, bf16[1024,128]{1,0:T(8,128)(2,1)S(1)}, bf16[1024,1024]{1,0:T(8,128)(2,1)S(1)}, bf16[1024,1024]{1,0:T(8,128)(2,1)S(1)}) custom-call(s32[1,1,4,256]{3,2,1,0:T(4,128)S(1)} %get-tuple-element.33.rows, bf16[1024,128]{1,0:T(8,128)(2,1)S(1)} %get-tuple-element.34.live_sign, ...), custom_call_target="tpu_custom_call" | custom-call | flops 100000000 | bytes 4000000 | tf_op jit(solution)/shard_map/pallas_call | solution.py:298
  19.0 0.4 collective-permute-done.3.r3
  19.5 2.0 %shard_map.97 = (bf16[1024,128]{1,0:T(8,128)(2,1)S(1)}, bf16[1024,128]{1,0:T(8,128)(2,1)S(1)}, bf16[256,128]{1,0:T(8,128)(2,1)S(1)}, bf16[256,128]{1,0:T(8,128)(...) custom-call(bf16[1024,1024]{1,0:T(8,128)(2,1)S(1)} %get-tuple-element.38.put, ...), custom_call_target="tpu_custom_call" | custom-call | flops 800000000 | bytes 4000000 | tf_op jit(solution)/shard_map/pallas_call | solution.py:303
  21.5 1.9 %collective-permute-start.4 = (bf16[256,128]{1,0:T(8,128)(2,1)S(1)}, bf16[256,128]{1,0:T(8,128)(2,1)S(1)}, u32[]{:S(2)}, u32[]{:S(2)}) collective-permute-start(bf16[256,128]{1,0:T(8,128)(2,1)S(1)} %get-tuple-element.51), channel_id=1, source_target_pairs={{0,8},{8,16},{16,24},{24,32},{32,40},{40,48},{48,56},{56,64},{64,7... | collective-permute-start | bytes 196616 | tf_op jit(solution)/shard_map/ppermute | solution.py:266
  23.4 5.8 %collective-permute-start.5 = (bf16[256,128]{1,0:T(8,128)(2,1)S(1)}, bf16[256,128]{1,0:T(8,128)(2,1)S(1)}, u32[]{:S(2)}, u32[]{:S(2)}) collective-permute-start(bf16[256,128]{1,0:T(8,128)(2,1)S(1)} %get-tuple-element.52), channel_id=1, source_target_pairs={{8,0},{16,8},{24,16},{32,24},{40,32},{48,40},{56,48},{64,56},{72,6... | collective-permute-start | bytes 196616 | tf_op jit(solution)/shard_map/ppermute | solution.py:267
  29.2 2.4 %collective-permute-start.6 = (bf16[256,128]{1,0:T(8,128)(2,1)S(1)}, bf16[256,128]{1,0:T(8,128)(2,1)S(1)}, u32[]{:S(2)}, u32[]{:S(2)}) collective-permute-start(bf16[256,128]{1,0:T(8,128)(2,1)S(1)} %get-tuple-element.53), channel_id=1, source_target_pairs={{0,1},{1,2},{2,3},{3,4},{4,5},{5,6},{6,7},{8,9},{9,10},{10,11},{11... | collective-permute-start | bytes 196616 | tf_op jit(solution)/shard_map/ppermute | solution.py:268
  31.6 5.0 %collective-permute-start.7 = (bf16[256,128]{1,0:T(8,128)(2,1)S(1)}, bf16[256,128]{1,0:T(8,128)(2,1)S(1)}, u32[]{:S(2)}, u32[]{:S(2)}) collective-permute-start(bf16[256,128]{1,0:T(8,128)(2,1)S(1)} %get-tuple-element.54), channel_id=1, source_target_pairs={{1,0},{2,1},{3,2},{4,3},{5,4},{6,5},{7,6},{9,8},{10,9},{11,10},{12... | collective-permute-start | bytes 196616 | tf_op jit(solution)/shard_map/ppermute | solution.py:269
  37.0 1.5 %collective-permute-done.7.r3 = bf16[256,128]{1,0:T(8,128)(2,1)S(1)} collective-permute-done((bf16[256,128]{1,0:T(8,128)(2,1)S(1)}, bf16[256,128]{1,0:T(8,128)(2,1)S(1)}, u32[]{:S(2)}, u32[]{:S(2)}) %collective-permute-start.7) | collective-permute-done | bytes 65568 | tf_op jit(solution)/shard_map/ppermute | solution.py:269
  38.5 2.0 %shard_map.98 = (bf16[1024,128]{1,0:T(8,128)(2,1)S(1)}, bf16[1024,128]{1,0:T(8,128)(2,1)S(1)}, bf16[256,128]{1,0:T(8,128)(2,1)S(1)}, bf16[256,128]{1,0:T(8,128)(...) custom-call(bf16[1024,1024]{1,0:T(8,128)(2,1)S(1)} %get-tuple-element.38.put, ...), custom_call_target="tpu_custom_call" | custom-call | flops 800000000 | bytes 4000000 | tf_op jit(solution)/shard_map/pallas_call | solution.py:303
  40.9 15.2 %all_to_all.15 = f32[64,4,128]{2,1,0:T(4,128)S(1)} all-to-all(f32[64,4,128]{2,1,0:T(4,128)S(1)} %bitcast.6), channel_id=1, replica_groups=mesh['z'=12,'x'=4,'core'=2,'y'=8] {'x','core','y'}, dimensions={0} | all-to-all | bytes 262144 | tf_op jit(solution)/shard_map/all_to_all | solution.py:277
  56.2 24.8 %all_to_all.16 = f32[12,4,128]{2,1,0:T(4,128)S(1)} all-to-all(f32[12,4,128]{2,1,0:T(4,128)S(1)} %broadcast_in_dim.8), channel_id=1, replica_groups=mesh['z'=12,'x'=4,'core'=2,'y'=8] {'z'}, dimensions={0} | all-to-all | bytes 49152 | tf_op jit(solution)/shard_map/all_to_all | solution.py:279
  81.0 0.7 broadcast_in_dim.9
  81.7 8.8 %all-to-all-start.2 = ((f32[64,4,128]{2,1,0:T(4,128)}), f32[64,4,128]{2,1,0:T(4,128)S(1)}, u32[]{:S(2)}, u32[]{:S(2)}) async-start(f32[64,4,128]{2,1,0:T(4,128)} %broadcast_in_dim.9), calls=%async_computation.2 | async-start | bytes 262144 | tf_op jit(solution)/shard_map/all_to_all | solution.py:281
  90.5 2.1 %collective-permute-start.8 = (bf16[256,128]{1,0:T(8,128)(2,1)S(1)}, bf16[256,128]{1,0:T(8,128)(2,1)S(1)}, u32[]{:S(2)}, u32[]{:S(2)}) collective-permute-start(bf16[256,128]{1,0:T(8,128)(2,1)S(1)} %get-tuple-element.55), channel_id=1, source_target_pairs={{0,8},{8,16},{16,24},{24,32},{32,40},{40,48},{48,56},{56,64},{64,7... | collective-permute-start | bytes 196616 | tf_op jit(solution)/shard_map/ppermute | solution.py:266
  92.6 5.6 %collective-permute-start.9 = (bf16[256,128]{1,0:T(8,128)(2,1)S(1)}, bf16[256,128]{1,0:T(8,128)(2,1)S(1)}, u32[]{:S(2)}, u32[]{:S(2)}) collective-permute-start(bf16[256,128]{1,0:T(8,128)(2,1)S(1)} %get-tuple-element.56), channel_id=1, source_target_pairs={{8,0},{16,8},{24,16},{32,24},{40,32},{48,40},{56,48},{64,56},{72,6... | collective-permute-start | bytes 196616 | tf_op jit(solution)/shard_map/ppermute | solution.py:267
  98.2 2.5 %collective-permute-start.10 = (bf16[256,128]{1,0:T(8,128)(2,1)S(1)}, bf16[256,128]{1,0:T(8,128)(2,1)S(1)}, u32[]{:S(2)}, u32[]{:S(2)}) collective-permute-start(bf16[256,128]{1,0:T(8,128)(2,1)S(1)} %get-tuple-element.57), channel_id=1, source_target_pairs={{0,1},{1,2},{2,3},{3,4},{4,5},{5,6},{6,7},{8,9},{9,10},{10,11},{11... | collective-permute-start | bytes 196616 | tf_op jit(solution)/shard_map/ppermute | solution.py:268
  100.7 4.8 %collective-permute-start.11 = (bf16[256,128]{1,0:T(8,128)(2,1)S(1)}, bf16[256,128]{1,0:T(8,128)(2,1)S(1)}, u32[]{:S(2)}, u32[]{:S(2)}) collective-permute-start(bf16[256,128]{1,0:T(8,128)(2,1)S(1)} %get-tuple-element.58), channel_id=1, source_target_pairs={{1,0},{2,1},{3,2},{4,3},{5,4},{6,5},{7,6},{9,8},{10,9},{11,10},{12... | collective-permute-start | bytes 196616 | tf_op jit(solution)/shard_map/ppermute | solution.py:269
  105.5 5.6 %shard_map.101.alpha = f32[128,128]{1,0:T(8,128)S(1)} custom-call(f32[64,4,128]{2,1,0:T(4,128)S(1)} %all-to-all-done.2.both), custom_call_target="tpu_custom_call" | custom-call | flops 100000000 | bytes 4000000 | tf_op jit(solution)/shard_map/pallas_call | solution.py:318
  111.1 2.8 %shard_map.102 = (f32[1024,128]{1,0:T(8,128)}, f32[1024,128]{1,0:T(8,128)}) custom-call(s32[1,1,4,256]{3,2,1,0:T(4,128)S(1)} %get-tuple-element.33.rows, bf16[256,128]{1,0:T(8,128)(2,1)S(1)} %collective-permute-done.8.r0, bf16[256,128]{1,0:T(8,128)(2,1)S(1)} %collective-permute-done.9.r1, bf16[256,128]{1,0:T(8,128)(2,1)S(1)} %collective-permute-done.10.r2, ...), custom_call_target="tpu_custom_call" | custom-call | flops 100000000 | bytes 4000000 | tf_op jit(solution)/shard_map/pallas_call | solution.py:320
  (17 shorter events, 0.8 us)
Async XLA Ops:
  2.8 16.2 %collective-permute-start = (bf16[256,128]{1,0:T(8,128)(2,1)S(1)}, bf16[256,128]{1,0:T(8,128)(2,1)S(1)}, u32[]{:S(2)}, u32[]{:S(2)}) collective-permute-start(bf16[256,128]{1,0:T(8,128)(2,1)S(1)} %get-tuple-element.46), channel_id=1, source_target_pairs={{0,8},{8,16},{16,24},{24,32},{32,40},{40,48},{48,56},{56,64},{64,7... | collective-permute-start | bytes 196616 | tf_op jit(solution)/shard_map/ppermute | solution.py:266
  4.8 14.3 %collective-permute-start.1 = (bf16[256,128]{1,0:T(8,128)(2,1)S(1)}, bf16[256,128]{1,0:T(8,128)(2,1)S(1)}, u32[]{:S(2)}, u32[]{:S(2)}) collective-permute-start(bf16[256,128]{1,0:T(8,128)(2,1)S(1)} %get-tuple-element.47), channel_id=1, source_target_pairs={{8,0},{16,8},{24,16},{32,24},{40,32},{48,40},{56,48},{64,56},{72,6... | collective-permute-start | bytes 196616 | tf_op jit(solution)/shard_map/ppermute | solution.py:267
  10.5 8.5 %collective-permute-start.2 = (bf16[256,128]{1,0:T(8,128)(2,1)S(1)}, bf16[256,128]{1,0:T(8,128)(2,1)S(1)}, u32[]{:S(2)}, u32[]{:S(2)}) collective-permute-start(bf16[256,128]{1,0:T(8,128)(2,1)S(1)} %get-tuple-element.48), channel_id=1, source_target_pairs={{0,1},{1,2},{2,3},{3,4},{4,5},{5,6},{6,7},{8,9},{9,10},{10,11},{11... | collective-permute-start | bytes 196616 | tf_op jit(solution)/shard_map/ppermute | solution.py:268
  13.1 6.4 %collective-permute-start.3 = (bf16[256,128]{1,0:T(8,128)(2,1)S(1)}, bf16[256,128]{1,0:T(8,128)(2,1)S(1)}, u32[]{:S(2)}, u32[]{:S(2)}) collective-permute-start(bf16[256,128]{1,0:T(8,128)(2,1)S(1)} %get-tuple-element.49), channel_id=1, source_target_pairs={{1,0},{2,1},{3,2},{4,3},{5,4},{6,5},{7,6},{9,8},{10,9},{11,10},{12... | collective-permute-start | bytes 196616 | tf_op jit(solution)/shard_map/ppermute | solution.py:269
  21.5 15.5 %collective-permute-start.4 = (bf16[256,128]{1,0:T(8,128)(2,1)S(1)}, bf16[256,128]{1,0:T(8,128)(2,1)S(1)}, u32[]{:S(2)}, u32[]{:S(2)}) collective-permute-start(bf16[256,128]{1,0:T(8,128)(2,1)S(1)} %get-tuple-element.51), channel_id=1, source_target_pairs={{0,8},{8,16},{16,24},{24,32},{32,40},{40,48},{48,56},{56,64},{64,7... | collective-permute-start | bytes 196616 | tf_op jit(solution)/shard_map/ppermute | solution.py:266
  23.4 13.5 %collective-permute-start.5 = (bf16[256,128]{1,0:T(8,128)(2,1)S(1)}, bf16[256,128]{1,0:T(8,128)(2,1)S(1)}, u32[]{:S(2)}, u32[]{:S(2)}) collective-permute-start(bf16[256,128]{1,0:T(8,128)(2,1)S(1)} %get-tuple-element.52), channel_id=1, source_target_pairs={{8,0},{16,8},{24,16},{32,24},{40,32},{48,40},{56,48},{64,56},{72,6... | collective-permute-start | bytes 196616 | tf_op jit(solution)/shard_map/ppermute | solution.py:267
  29.2 7.8 %collective-permute-start.6 = (bf16[256,128]{1,0:T(8,128)(2,1)S(1)}, bf16[256,128]{1,0:T(8,128)(2,1)S(1)}, u32[]{:S(2)}, u32[]{:S(2)}) collective-permute-start(bf16[256,128]{1,0:T(8,128)(2,1)S(1)} %get-tuple-element.53), channel_id=1, source_target_pairs={{0,1},{1,2},{2,3},{3,4},{4,5},{5,6},{6,7},{8,9},{9,10},{10,11},{11... | collective-permute-start | bytes 196616 | tf_op jit(solution)/shard_map/ppermute | solution.py:268
  31.6 6.9 %collective-permute-start.7 = (bf16[256,128]{1,0:T(8,128)(2,1)S(1)}, bf16[256,128]{1,0:T(8,128)(2,1)S(1)}, u32[]{:S(2)}, u32[]{:S(2)}) collective-permute-start(bf16[256,128]{1,0:T(8,128)(2,1)S(1)} %get-tuple-element.54), channel_id=1, source_target_pairs={{1,0},{2,1},{3,2},{4,3},{5,4},{6,5},{7,6},{9,8},{10,9},{11,10},{12... | collective-permute-start | bytes 196616 | tf_op jit(solution)/shard_map/ppermute | solution.py:269
  81.7 23.8 %all-to-all-start.2 = ((f32[64,4,128]{2,1,0:T(4,128)}), f32[64,4,128]{2,1,0:T(4,128)S(1)}, u32[]{:S(2)}, u32[]{:S(2)}) async-start(f32[64,4,128]{2,1,0:T(4,128)} %broadcast_in_dim.9), calls=%async_computation.2 | async-start | bytes 262144 | tf_op jit(solution)/shard_map/all_to_all | solution.py:281
  90.5 20.5 %collective-permute-start.8 = (bf16[256,128]{1,0:T(8,128)(2,1)S(1)}, bf16[256,128]{1,0:T(8,128)(2,1)S(1)}, u32[]{:S(2)}, u32[]{:S(2)}) collective-permute-start(bf16[256,128]{1,0:T(8,128)(2,1)S(1)} %get-tuple-element.55), channel_id=1, source_target_pairs={{0,8},{8,16},{16,24},{24,32},{32,40},{40,48},{48,56},{56,64},{64,7... | collective-permute-start | bytes 196616 | tf_op jit(solution)/shard_map/ppermute | solution.py:266
  92.6 18.4 %collective-permute-start.9 = (bf16[256,128]{1,0:T(8,128)(2,1)S(1)}, bf16[256,128]{1,0:T(8,128)(2,1)S(1)}, u32[]{:S(2)}, u32[]{:S(2)}) collective-permute-start(bf16[256,128]{1,0:T(8,128)(2,1)S(1)} %get-tuple-element.56), channel_id=1, source_target_pairs={{8,0},{16,8},{24,16},{32,24},{40,32},{48,40},{56,48},{64,56},{72,6... | collective-permute-start | bytes 196616 | tf_op jit(solution)/shard_map/ppermute | solution.py:267
  98.2 12.9 %collective-permute-start.10 = (bf16[256,128]{1,0:T(8,128)(2,1)S(1)}, bf16[256,128]{1,0:T(8,128)(2,1)S(1)}, u32[]{:S(2)}, u32[]{:S(2)}) collective-permute-start(bf16[256,128]{1,0:T(8,128)(2,1)S(1)} %get-tuple-element.57), channel_id=1, source_target_pairs={{0,1},{1,2},{2,3},{3,4},{4,5},{5,6},{6,7},{8,9},{9,10},{10,11},{11... | collective-permute-start | bytes 196616 | tf_op jit(solution)/shard_map/ppermute | solution.py:268
  100.7 10.4 %collective-permute-start.11 = (bf16[256,128]{1,0:T(8,128)(2,1)S(1)}, bf16[256,128]{1,0:T(8,128)(2,1)S(1)}, u32[]{:S(2)}, u32[]{:S(2)}) collective-permute-start(bf16[256,128]{1,0:T(8,128)(2,1)S(1)} %get-tuple-element.58), channel_id=1, source_target_pairs={{1,0},{2,1},{3,2},{4,3},{5,4},{6,5},{7,6},{9,8},{10,9},{11,10},{12... | collective-permute-start | bytes 196616 | tf_op jit(solution)/shard_map/ppermute | solution.py:269
